TPU v7x, 128 devices: a whole 4x4x4 slice. The times are simulated.
128 devices in a mesh: row: 64 (over z, y_lo, x, core), chan: 2 (over y_hi).
Axes of the slice: x: 4, y: 4 (y_hi: 2, y_lo: 2; y = y_hi * 2 + y_lo), z: 4, core: 2. Of those that a mesh axis runs over, the one named last changes fastest.
Arguments:
- sky_image: float32 [2, 4096, 4096], P('chan', 'row'), may hold values from -6 to 6
- fourier_dual: float32 [2, 2, 4096, 4096], P(None, 'chan', 'row'), may hold values from -6 to 6
- visibilities: float32 [2, 2, 4096, 4096], P(None, 'chan', 'row'), may hold values from -18 to 18
- weights: float32 [2, 4096, 4096], P('chan', 'row'), may hold values from 0.1 to 1
- radius: float32 [2], P('chan'), may hold values from 0.2 to 0.6
- wavelet_dual: float32 [2, 4096, 4096], P(None, ('row', 'chan')), may hold values from -6 to 6
- reweight: float32 [4096, 4096], P(('row', 'chan')), may hold values from 0.3 to 3
Outputs:
- image_new: float32 [2, 4096, 4096], P('chan', 'row')
- fourier_new: float32 [2, 2, 4096, 4096], P(None, 'chan', 'row')
- wavelet_new: float32 [2, 4096, 4096], P(None, ('row', 'chan'))
All inputs are finite; a program needn't handle non-finite values.
Results may differ from a plain program's by a relative error of at most 0.000084.
Values sent between devices are 32-bit elements; how exact they have to be, the bound alone decides.
A program may use at most 128 MiB of HBM per device.

v0:
```python
import math

import jax
import jax.numpy as jnp
import numpy as np
from jax import lax
from jax.experimental import pallas as pl
from jax.experimental.pallas import tpu as pltpu
from jax.sharding import PartitionSpec as P

data_step = 0.8
primal_step = 0.5
low_taps = (0.0625, 0.25, 0.375, 0.25, 0.0625)
high_taps = (-0.1, -0.3, 0.7, -0.2, -0.1)
low_reverse = (0.0625, 0.25, 0.375, 0.25, 0.0625)
high_reverse = (-0.1, -0.2, 0.7, -0.3, -0.1)

SIDE = 4096
RADIX = 32
WIDE = 128


def over_copies(array, axis):
    count = lax.axis_size(axis)
    sent = jnp.broadcast_to(array[None], (count, *array.shape))
    return lax.all_to_all(sent, axis, 0, 0, tiled=True).sum(axis=0)


def extended_2(array, sides, width):
    edges = {}
    for axis, dim in sides:
        count, length = (lax.axis_size(axis), array.shape[dim])
        up = [(i, (i + 1) % count) for i in range(count - 1)]
        last = lax.slice_in_dim(array, length - width, length, axis=dim)
        first = lax.slice_in_dim(array, 0, width, axis=dim)
        edges[dim] = (
            lax.ppermute(last, axis, up),
            lax.ppermute(first, axis, [(b, a) for a, b in up]),
        )
    for _, dim in sides:
        low, high = edges[dim]
        array = jnp.concatenate([low, array, high], axis=dim)
    return array


def filter_rows(extended, filter_taps):
    count_rows = extended.shape[1] - 4
    total = filter_taps[0] * extended[:, 0:count_rows]
    for offset in range(1, 5):
        total = total + filter_taps[offset] * extended[:, offset : offset + count_rows]
    return total


def filter_columns(values, filter_taps):
    count_cols = values.shape[2]
    padded = jnp.pad(values, ((0, 0), (0, 0), (2, 2)))
    total = filter_taps[0] * padded[:, :, 0:count_cols]
    for offset in range(1, 5):
        total = total + filter_taps[offset] * padded[:, :, offset : offset + count_cols]
    return total


def analysis(extended, low_set, high_set):
    return filter_columns(filter_rows(extended, high_set), low_set) + filter_columns(
        filter_rows(extended, low_set), high_set
    )


def soft_dual(combined, threshold):
    magnitude = jnp.sqrt(jnp.sum(combined * combined, axis=0))
    return combined * (threshold / jnp.maximum(magnitude, threshold))


def c_add(a, b):
    re = a[0] + b[0]
    if a[1] is None:
        return (re, b[1])
    return (re, a[1] if b[1] is None else a[1] + b[1])


def c_sub(a, b):
    re = a[0] - b[0]
    if a[1] is None:
        return (re, None if b[1] is None else -b[1])
    return (re, a[1] if b[1] is None else a[1] - b[1])


def c_turn(a, k, n, orient):
    re, im = a
    if k == 0:
        return a
    if 4 * k == n:
        if im is None:
            return (None, re if orient > 0 else -re)
        return (-im, re) if orient > 0 else (im, -re)
    cos, sin = math.cos(2 * math.pi * k / n), orient * math.sin(2 * math.pi * k / n)
    if im is None:
        return (re * cos, re * sin)
    if 8 * k == n:
        return ((re - im) * cos, (re + im) * cos) if orient > 0 else ((re + im) * cos, (im - re) * cos)
    if 8 * k == 3 * n:
        c = -cos
        return ((-re - im) * c, (re - im) * c) if orient > 0 else ((im - re) * c, (-re - im) * c)
    return (re * cos - im * sin, re * sin + im * cos)


def short_fft(items, orient):
    n = len(items)
    if n == 1:
        return list(items)
    even = short_fft(items[0::2], orient)
    odd = short_fft(items[1::2], orient)
    low, high = [], []
    for k in range(n // 2):
        if even[k][1] is None and odd[k][1] is None and 4 * k == n:
            low.append((even[k][0], orient * odd[k][0]))
            high.append((even[k][0], -orient * odd[k][0]))
            continue
        turned = c_turn(odd[k], k, n, orient)
        low.append(c_add(even[k], turned))
        high.append(c_sub(even[k], turned))
    return low + high


def dft_matrix(orient):
    idx = np.arange(WIDE)
    angle = 2 * np.pi * ((idx[:, None] * idx[None, :]) % WIDE) / WIDE
    cos, sin = np.cos(angle) / 64.0, orient * np.sin(angle) / 64.0
    return np.block([[cos, sin], [-sin, cos]])


def halves_first(matrix_rows):
    order = np.arange(WIDE).reshape(64, 2).T.reshape(-1)
    return np.concatenate([matrix_rows[:WIDE][order], matrix_rows[WIDE:][order]])


def high_low(matrix):

    bf = np.asarray(matrix, np.float32).astype(jnp.bfloat16)
    low = (np.asarray(matrix) - bf.astype(np.float64)).astype(jnp.bfloat16)
    return (jnp.asarray(np.stack([bf, low])),)


def twiddle(orient):
    angle = 2 * np.pi * (np.arange(RADIX)[:, None] * np.arange(WIDE)[None, :]) / SIDE
    return jnp.asarray(np.stack([np.cos(angle), orient * np.sin(angle)]), jnp.float32)


def split_two(x):
    high = x.astype(jnp.bfloat16)
    return high, (x - high.astype(jnp.float32)).astype(jnp.bfloat16)


def product(dims, a_pair, b_pair):
    def one(a, b):
        return lax.dot_general(a, b, (dims, ((), ())), preferred_element_type=jnp.float32)

    return one(a_pair[0], b_pair[0]) + (one(a_pair[1], b_pair[0]) + one(a_pair[0], b_pair[1]))


def spread(matrix_ref, block):
    return product(((1,), (1,)), (matrix_ref[0], matrix_ref[1]), split_two(block))


def gather(block, matrix_ref):
    return product(((0,), (0,)), split_two(block), (matrix_ref[0], matrix_ref[1]))


def c_mul(a, b_re, b_im):
    return (a[0] * b_re - a[1] * b_im, a[0] * b_im + a[1] * b_re)


def rows_forward(x_ref, tw_ref, matrix_ref, out_ref, held):
    def short(at, _):
        items = [(x_ref[at, p], None) for p in range(RADIX)]
        done = short_fft(items, -1)
        a_hi, a_mid = at // 2, at % 2
        for q in range(RADIX):
            value = done[q]
            if value[1] is None:
                re = value[0] * tw_ref[0, pl.ds(q, 1), :]
                im = value[0] * tw_ref[1, pl.ds(q, 1), :]
            else:
                re, im = c_mul(value, tw_ref[0, pl.ds(q, 1), :], tw_ref[1, pl.ds(q, 1), :])
            row = pl.ds(pl.multiple_of((q % 8) * 16 + a_mid * 8, 8), 8)
            held[(q // 8) * 4 + a_hi, row, 0:WIDE] = re
            held[(q // 8) * 4 + a_hi, row, WIDE:] = im
        return 0

    lax.fori_loop(0, 8, short, 0)

    def long(block, _):
        q_hi, a_hi = block // 4, block % 4
        result = spread(matrix_ref, held[block])
        for c in range(2):
            for e in range(2):
                for d in range(0, 64, 8):
                    start = d * 64 + c * 32 + e * 4 + a_hi * 8 + q_hi
                    m = c * 128 + e * 64 + d
                    out_ref[pl.ds(start, 8, stride=64), :] = result[m : m + 8]
        return 0

    lax.fori_loop(0, 16, long, 0)


def columns_both(
    in_ref, dual_ref, vis_ref, weight_ref, tw_ref, to_ref, back_ref,
    resid_ref, out_ref, sums_ref, wide, held,
):
    def long(block, _):
        l_hi, q_hi = block // 8, block % 8
        rows = []
        for c in range(2):
            for jh in range(2):
                rows.append(in_ref[pl.ds(c * 32 + jh * 16 + l_hi * 8 + q_hi, 64, stride=64), :])
        result = gather(jnp.concatenate(rows), to_ref)
        for q_lo in range(8):
            row = pl.ds(pl.multiple_of((q_hi * 8 + q_lo) * 32 + l_hi * 16, 8), 16)
            wide[0, row, :] = result[q_lo * 16 : q_lo * 16 + 16, 0:WIDE]
            wide[1, row, :] = result[q_lo * 16 : q_lo * 16 + 16, WIDE:]
        return 0

    lax.fori_loop(0, 16, long, 0)
    sums_ref[...] = jnp.zeros_like(sums_ref)

    def short(q_hi, _):
        items = []
        for l in range(RADIX):
            row = pl.ds(q_hi * 256 + l, 8, stride=32)
            items.append(
                c_mul((wide[0, row, :], wide[1, row, :]), tw_ref[0, pl.ds(l, 1), :], tw_ref[1, pl.ds(l, 1), :])
            )
        freq = short_fft(items, -1)
        total = sums_ref[0]
        total_vis = sums_ref[1]
        items = []
        for v in range(RADIX):
            weight = weight_ref[q_hi, v]
            vis_re, vis_im = vis_ref[0, q_hi, v], vis_ref[1, q_hi, v]
            re = dual_ref[0, q_hi, v] * (1.0 / data_step) + weight * freq[v][0] - vis_re
            im = dual_ref[1, q_hi, v] * (1.0 / data_step) + weight * freq[v][1] - vis_im
            total = total + (re * re + im * im)
            total_vis = total_vis + (vis_re * vis_re + vis_im * vis_im)
            resid_ref[0, q_hi, v] = re
            resid_ref[1, q_hi, v] = im
            items.append((weight * re, weight * im))
        sums_ref[0] = total
        sums_ref[1] = total_vis
        done = short_fft(items, 1)
        for l in range(RADIX):
            re, im = c_mul(done[l], tw_ref[0, pl.ds(l, 1), :], -tw_ref[1, pl.ds(l, 1), :])
            row = pl.ds((l % 16) * 8, 8)
            held[(l // 16) * 8 + q_hi, row, 0:WIDE] = re
            held[(l // 16) * 8 + q_hi, row, WIDE:] = im
        return 0

    lax.fori_loop(0, 8, short, 0)

    def long_back(block, _):
        l_hi, q_hi = block // 8, block % 8
        result = spread(back_ref, held[block])
        for c in range(2):
            for jh in range(2):
                for s in range(0, 64, 8):
                    start = s * 64 + c * 32 + jh * 16 + l_hi * 8 + q_hi
                    m = c * 128 + jh * 64 + s
                    out_ref[pl.ds(start, 8, stride=64), :] = result[m : m + 8]
        return 0

    lax.fori_loop(0, 16, long_back, 0)


def rows_back(shrink_ref, in_ref, x_ref, adjoint_ref, tw_ref, matrix_ref, out_ref, wide):
    def long(block, _):
        a_hi, q_hi = block // 4, block % 4
        rows = []
        for c in range(2):
            for e in range(2):
                rows.append(in_ref[pl.ds(c * 32 + a_hi * 8 + e * 4 + q_hi, 64, stride=64), :])
        result = gather(jnp.concatenate(rows), matrix_ref)
        for a_lo in range(16):
            row = pl.ds(pl.multiple_of((a_hi * 16 + a_lo) * 32 + q_hi * 8, 8), 8)
            wide[0, row, :] = result[a_lo * 8 : a_lo * 8 + 8, 0:WIDE]
            wide[1, row, :] = result[a_lo * 8 : a_lo * 8 + 8, WIDE:]
        return 0

    lax.fori_loop(0, 16, long, 0)
    shrink = shrink_ref[0]

    def short(at, _):
        items = []
        for q in range(RADIX):
            row = pl.ds(at * 256 + q, 8, stride=32)
            items.append(
                c_mul((wide[0, row, :], wide[1, row, :]), tw_ref[0, pl.ds(q, 1), :], -tw_ref[1, pl.ds(q, 1), :])
            )
        done = short_fft(items, 1)
        for p in range(RADIX):
            step = done[p][0] * shrink + adjoint_ref[at, p]
            out_ref[at, p] = jnp.maximum(x_ref[at, p] - primal_step * step, 0.0)
        return 0

    lax.fori_loop(0, 8, short, 0)


def tiles(array):
    lead = array.shape[:-2]
    array = array.reshape(lead + (8, 8, 32, 128))
    n = len(lead)
    return array.transpose(tuple(range(n)) + (n, n + 2, n + 1, n + 3))


def untiles(array):
    n = array.ndim - 4
    array = array.transpose(tuple(range(n)) + (n, n + 2, n + 1, n + 3))
    return array.reshape(array.shape[:n] + (64, SIDE))


TILES = (8, 32, 8, 128)
VMEM_SPEC = pl.BlockSpec(memory_space=pltpu.VMEM)
F32 = jnp.float32


def per_device(sky_image, fourier_dual, visibilities, weights, radius, wavelet_dual, reweight):
    tw = twiddle(-1.0)
    forward, backward = dft_matrix(-1.0), dft_matrix(1.0)
    spread_rows = high_low(halves_first(forward.T))[0]
    gather_cols = high_low(halves_first(forward))[0]
    spread_cols = high_low(halves_first(backward.T))[0]
    gather_rows = high_low(halves_first(backward))[0]
    params = pltpu.CompilerParams(vmem_limit_bytes=48 << 20)

    x_tiles = tiles(sky_image[0])
    sent = pl.pallas_call(
        rows_forward,
        out_shape=jax.ShapeDtypeStruct((4096, 128), F32),
        in_specs=[VMEM_SPEC] * 3,
        out_specs=VMEM_SPEC,
        scratch_shapes=[pltpu.VMEM((16, 128, 256), F32)],
        compiler_params=params,
        cost_estimate=pl.CostEstimate(flops=8 << 27, bytes_accessed=4 << 20, transcendentals=0),
    )(x_tiles, tw, spread_rows)
    arrived = lax.all_to_all(sent.reshape(64, 64, 128), "row", 0, 0, tiled=True).reshape(4096, 128)
    resid, outgoing, sums = pl.pallas_call(
        columns_both,
        out_shape=(
            jax.ShapeDtypeStruct((2, *TILES), F32),
            jax.ShapeDtypeStruct((4096, 128), F32),
            jax.ShapeDtypeStruct((2, 8, 128), F32),
        ),
        in_specs=[VMEM_SPEC] * 7,
        out_specs=(VMEM_SPEC,) * 3,
        scratch_shapes=[pltpu.VMEM((2, 2048, 128), F32), pltpu.VMEM((16, 128, 256), F32)],
        compiler_params=params,
        cost_estimate=pl.CostEstimate(flops=16 << 27, bytes_accessed=12 << 20, transcendentals=0),
    )(
        arrived, tiles(fourier_dual[:, 0]), tiles(visibilities[:, 0]), tiles(weights[0]), tw,
        gather_cols, spread_cols,
    )
    returned = lax.all_to_all(outgoing.reshape(64, 64, 128), "row", 0, 0, tiled=True).reshape(4096, 128)
    norms = over_copies(jnp.sum(sums, axis=(1, 2)), "row")
    shrink = data_step * (1.0 - radius * jnp.sqrt(norms[1]) / jnp.sqrt(norms[0]))
    fourier_new = untiles(resid * shrink[0])[:, None]

    facet_image = lax.all_to_all(sky_image, "chan", split_axis=1, concat_axis=0, tiled=True)
    channels = facet_image.shape[0]
    rows_facet = facet_image.shape[1]
    bundle = jnp.concatenate([facet_image, wavelet_dual, reweight[None]], axis=0)
    extended = extended_2(bundle, ((("row", "chan"), 1),), 4)
    combined = extended[channels : 2 * channels, 2:-2] + analysis(
        extended[:channels], low_taps, high_taps
    )
    offset_row = lax.axis_index(("row", "chan")) * rows_facet - 2
    positions = offset_row + jnp.arange(rows_facet + 4, dtype=jnp.int32)
    total_rows = rows_facet * lax.axis_size(("row", "chan"))
    inside = (positions >= 0) & (positions < total_rows)
    threshold = jnp.where(inside[:, None], extended[2 * channels, 2:-2], 1.0)
    wide_new = jnp.where(inside[None, :, None], soft_dual(combined, threshold), 0.0)
    wavelet_new = wide_new[:, 2:-2]
    adjoint = analysis(wide_new, low_reverse, high_reverse)
    adjoint_rows = lax.all_to_all(adjoint, "chan", split_axis=0, concat_axis=1, tiled=True)

    image = pl.pallas_call(
        rows_back,
        out_shape=jax.ShapeDtypeStruct(TILES, F32),
        in_specs=[pl.BlockSpec(memory_space=pltpu.SMEM)] + [VMEM_SPEC] * 5,
        out_specs=VMEM_SPEC,
        scratch_shapes=[pltpu.VMEM((2, 2048, 128), F32)],
        compiler_params=params,
        cost_estimate=pl.CostEstimate(flops=8 << 27, bytes_accessed=5 << 20, transcendentals=0),
    )(shrink, returned, x_tiles, tiles(adjoint_rows[0]), tw, gather_rows)
    return (untiles(image)[None], fourier_new, wavelet_new)


def solution(mesh):
    in_specs = (
        P("chan", "row", None),
        P(None, "chan", "row", None),
        P(None, "chan", "row", None),
        P("chan", "row", None),
        P("chan"),
        P(None, ("row", "chan"), None),
        P(("row", "chan"), None),
    )
    out_specs = (
        P("chan", "row", None),
        P(None, "chan", "row", None),
        P(None, ("row", "chan"), None),
    )
    return jax.shard_map(
        per_device, mesh=mesh, in_specs=in_specs, out_specs=out_specs, check_vma=False
    )
```

profile of v0, /device:TPU:1, one launch (start us, length us, event | category | flops | bytes accessed | tf_op | source)
XLA Modules:
  0.0 169.3 jit_solution(16172797613024100666)
XLA Ops:
  0.6 2.3 %copy.36 = f32[1,64,4096]{2,0,1:T(1,128)S(1)} copy(f32[1,64,4096]{2,1,0:T(8,128)} %param.12) | data formatting | bytes 2097152 | tf_op args[0]
  2.9 19.0 %all_to_all.37 = f32[1,64,4096]{2,0,1:T(1,128)S(1)} all-to-all(f32[1,64,4096]{2,0,1:T(1,128)S(1)} %copy.36), channel_id=1, replica_groups=mesh['row'=64,'chan'=2] {'chan'}, dimensions={1} | all-to-all | bytes 2097152 | tf_op jit(solution)/shard_map/all_to_all | solution.py:365
  22.0 0.6 copy.44
  22.6 0.6 copy-done.9
  23.5 1.0 copy.37
  24.5 2.2 %collective-permute-start = (f32[5,4,4096]{2,0,1:T(8,128)}, f32[5,4,4096]{2,0,1:T(8,128)}, u32[]{:S(2)}, u32[]{:S(2)}) collective-permute-start(f32[5,4,4096]{2,0,1:T(8,128)} %copy.37), channel_id=1, source_target_pairs={{0,1},{1,2},{2,3},{3,4},{4,5},{5,6},{6,7},{7,8},{8,9},{9,10},{10,1... | collective-permute-start | bytes 983048 | tf_op jit(solution)/shard_map/ppermute | solution.py:37
  26.7 1.0 copy.38
  27.7 4.9 %collective-permute-start.1 = (f32[5,4,4096]{2,0,1:T(8,128)}, f32[5,4,4096]{2,0,1:T(8,128)}, u32[]{:S(2)}, u32[]{:S(2)}) collective-permute-start(f32[5,4,4096]{2,0,1:T(8,128)} %copy.38), channel_id=1, source_target_pairs={{1,0},{2,1},{3,2},{4,3},{5,4},{6,5},{7,6},{8,7},{9,8},{10,9},{11,1... | collective-permute-start | bytes 983048 | tf_op jit(solution)/shard_map/ppermute | solution.py:38
  32.6 7.5 %shard_map.139 = f32[4096,128]{1,0:T(8,128)} custom-call(f32[8,32,8,128]{3,2,1,0:T(8,128)S(1)} %bitcast.34, f32[2,32,128]{2,1,0:T(8,128)S(1)} %copy-done.6, bf16[2,256,256]{2,1,0:T(8,128)(2,1)S(1)} %copy-done.5), custom_call_target="tpu_custom_call" | custom-call | flops 1073741824 | bytes 4194304 | tf_op jit(solution)/shard_map/pallas_call | solution.py:334
  40.1 11.4 %all-to-all-start = ((f32[64,64,128]{2,1,0:T(8,128)}), f32[64,64,128]{2,1,0:T(8,128)}, u32[]{:S(2)}, u32[]{:S(2)}) async-start(f32[64,64,128]{2,1,0:T(8,128)} %bitcast.2), calls=%async_computation | async-start | bytes 4194304 | tf_op jit(solution)/shard_map/all_to_all | solution.py:343
  51.5 1.3 copy.39
  53.2 1.3 copy.40
  55.0 0.8 multiply_add_fusion.1
  55.7 0.8 multiply_add_fusion
  56.5 2.8 %multiply_reduce_fusion = (f32[36,4096]{1,0:T(8,128)S(1)}, f32[2,36,4096]{2,1,0:T(8,128)S(1)}) fusion(f32[2,36,4096]{2,1,0:T(8,128)S(1)} %multiply_add_fusion, f32[2,36,4096]{2,1,0:T(8,128)S(1)} %multiply_add_fusion.1, f32[5,40,4096]{2,1,0:T(8,128)S(1)} %pad_maximum_fusion), kind=kLoop, calls=%fused_computation.10 | loop fusion | flops 6340608 | bytes 5308416 | tf_op jit(solution)/shard_map/reduce_sum | solution.py:70
  59.8 0.6 multiply_add_fusion.3
  60.4 0.5 multiply_add_fusion.2
  61.4 3.2 %add_add_fusion = f32[2,32,4096]{2,1,0:T(8,128)} fusion(f32[2,32,4096]{2,1,0:T(8,128)S(1)} %multiply_add_fusion.2, f32[2,32,4096]{2,1,0:T(8,128)S(1)} %get-tuple-element.12), kind=kLoop, calls=%fused_computation.17 | loop fusion | flops 4980736 | bytes 3145728 | tf_op jit(solution)/shard_map/add | solution.py:64
  64.6 16.1 %all-to-all-done = f32[64,64,128]{2,1,0:T(8,128)} async-done(((f32[64,64,128]{2,1,0:T(8,128)}), f32[64,64,128]{2,1,0:T(8,128)}, u32[]{:S(2)}, u32[]{:S(2)}) %all-to-all-start) | async-done | bytes 2097184 | tf_op jit(solution)/shard_map/all_to_all | solution.py:343
  80.7 3.6 %all-to-all-start.4 = ((f32[2,32,4096]{2,1,0:T(8,128)}), f32[2,32,4096]{2,1,0:T(8,128)S(1)}, u32[]{:S(2)}, u32[]{:S(2)}) async-start(f32[2,32,4096]{2,1,0:T(8,128)} %add_add_fusion), calls=%async_computation.4 | async-start | bytes 2097152 | tf_op jit(solution)/shard_map/all_to_all | solution.py:381
  84.3 1.2 copy-done.7
  85.5 16.8 %shard_map.140 = (f32[2,8,32,8,128]{4,3,2,1,0:T(8,128)S(1)}, f32[4096,128]{1,0:T(8,128)S(1)}, f32[2,8,128]{2,1,0:T(8,128)S(1)}) custom-call(f32[4096,128]{1,0:T(8,128)} %bitcast.3.in_ref, f32[2,8,32,8,128]{4,3,2,1,0:T(8,128)} %bitcast.48, f32[2,8,32,8,128]{4,3,2,1,0:T(8,128)} %bitcast.49, f32[8,32,8,128]{3,2,1,0:T(8,128)S(1)} %bitcast.38, ...), custom_call_target="tpu_custom_call" | custom-call | flops 2147483648 | bytes 12582912 | tf_op jit(solution)/shard_map/pallas_call | solution.py:344
  102.4 1.3 copy-done.3
  103.7 1.3 copy-done.4
  105.1 1.0 copy-done.1
  106.1 19.7 %all_to_all.38 = f32[64,1,2]{2,1,0:T(1,128)S(1)} all-to-all(f32[64,1,2]{2,1,0:T(1,128)S(1)} %broadcast_in_dim.36), channel_id=1, replica_groups=mesh['row'=64,'chan'=2] {'row'}, dimensions={0} | all-to-all | bytes 1024 | tf_op jit(solution)/shard_map/all_to_all | solution.py:26
  125.8 4.8 %all-to-all-start.2 = ((f32[64,64,128]{2,1,0:T(8,128)}), f32[64,64,128]{2,1,0:T(8,128)S(1)}, u32[]{:S(2)}, u32[]{:S(2)}) async-start(f32[64,64,128]{2,1,0:T(8,128)} %bitcast.37), calls=%async_computation.2 | async-start | bytes 4194304 | tf_op jit(solution)/shard_map/all_to_all | solution.py:360
  131.3 0.6 fusion.5
  133.3 3.1 %multiply_bitcast_fusion = f32[2,1,64,4096]{3,2,1,0:T(8,128)} fusion(f32[2,8,32,8,128]{4,3,2,1,0:T(8,128)} %copy-done.3, f32[]{:T(128)} %bitcast.19), kind=kLoop, calls=%fused_computation.1 | loop fusion | flops 524288 | bytes 4194308 | tf_op jit(solution)/shard_map/broadcast_in_dim;reshape | solution.py:363
  136.4 23.6 %all-to-all-done.2 = f32[64,64,128]{2,1,0:T(8,128)S(1)} async-done(((f32[64,64,128]{2,1,0:T(8,128)}), f32[64,64,128]{2,1,0:T(8,128)S(1)}, u32[]{:S(2)}, u32[]{:S(2)}) %all-to-all-start.2) | async-done | bytes 2097184 | tf_op jit(solution)/shard_map/all_to_all | solution.py:360
  160.1 1.2 copy-done.2
  161.3 8.1 %shard_map.141 = f32[8,32,8,128]{3,2,1,0:T(8,128)} custom-call(f32[1]{0:T(128)} %mul.153.shrink_ref, f32[4096,128]{1,0:T(8,128)S(1)} %bitcast.33, f32[8,32,8,128]{3,2,1,0:T(8,128)S(1)} %bitcast.35, f32[8,32,8,128]{3,2,1,0:T(8,128)S(1)} %bitcast.36, f32[2,32,128]{2,1,0:T(8,128)S(1)} %copy-done.6, bf16[2,256,256]{2,1,0:T(8,128)(2,1)S(1)} %copy-done.5), custom_call_target="tpu_custom_call" | custom-call | flops 1073741824 | bytes 5242880 | tf_op jit(solution)/shard_map/pallas_call | solution.py:383
  (31 shorter events, 2.4 us)
Async XLA Ops:
  22.0 1.2 copy-start.9
  22.0 1.4 copy-start.10
  23.5 9.1 %copy-start = (f32[1,64,4096]{2,1,0:T(8,128)S(1)}, f32[1,64,4096]{2,1,0:T(8,128)}, u32[]{:S(2)}) copy-start(f32[1,64,4096]{2,1,0:T(8,128)} %param.12) | copy-start | bytes 3145732
  23.5 9.1 %copy-start.5 = (bf16[2,256,256]{2,1,0:T(8,128)(2,1)S(1)}, bf16[2,256,256]{2,1,0:T(8,128)(2,1)}, u32[]{:S(2)}) copy-start(bf16[2,256,256]{2,1,0:T(8,128)(2,1)} %constant.19.clone.matrix_ref) | copy-start | bytes 786436
  23.5 9.1 %copy-start.6 = (f32[2,32,128]{2,1,0:T(8,128)S(1)}, f32[2,32,128]{2,1,0:T(8,128)}, u32[]{:S(2)}) copy-start(f32[2,32,128]{2,1,0:T(8,128)} %constant.18.clone.tw_ref) | copy-start | bytes 98308
  24.5 27.0 %collective-permute-start = (f32[5,4,4096]{2,0,1:T(8,128)}, f32[5,4,4096]{2,0,1:T(8,128)}, u32[]{:S(2)}, u32[]{:S(2)}) collective-permute-start(f32[5,4,4096]{2,0,1:T(8,128)} %copy.37), channel_id=1, source_target_pairs={{0,1},{1,2},{2,3},{3,4},{4,5},{5,6},{6,7},{7,8},{8,9},{9,10},{10,1... | collective-permute-start | bytes 983048 | tf_op jit(solution)/shard_map/ppermute | solution.py:37
  27.7 25.6 %collective-permute-start.1 = (f32[5,4,4096]{2,0,1:T(8,128)}, f32[5,4,4096]{2,0,1:T(8,128)}, u32[]{:S(2)}, u32[]{:S(2)}) collective-permute-start(f32[5,4,4096]{2,0,1:T(8,128)} %copy.38), channel_id=1, source_target_pairs={{1,0},{2,1},{3,2},{4,3},{5,4},{6,5},{7,6},{8,7},{9,8},{10,9},{11,1... | collective-permute-start | bytes 983048 | tf_op jit(solution)/shard_map/ppermute | solution.py:38
  40.1 40.6 %all-to-all-start = ((f32[64,64,128]{2,1,0:T(8,128)}), f32[64,64,128]{2,1,0:T(8,128)}, u32[]{:S(2)}, u32[]{:S(2)}) async-start(f32[64,64,128]{2,1,0:T(8,128)} %bitcast.2), calls=%async_computation | async-start | bytes 4194304 | tf_op jit(solution)/shard_map/all_to_all | solution.py:343
  51.5 3.0 %copy-start.11 = (f32[32,4096]{1,0:T(8,128)S(1)}, f32[32,4096]{1,0:T(8,128)}, u32[]{:S(2)}) copy-start(f32[32,4096]{1,0:T(8,128)} %param.18) | copy-start | bytes 1572868
  60.4 1.0 copy-start.12
  64.6 19.7 %copy-start.8 = (bf16[2,256,256]{2,1,0:T(8,128)(2,1)S(1)}, bf16[2,256,256]{2,1,0:T(8,128)(2,1)}, u32[]{:S(2)}) copy-start(bf16[2,256,256]{2,1,0:T(8,128)(2,1)} %constant.20.clone.to_ref.back_ref) | copy-start | bytes 786436
  80.7 24.5 %all-to-all-start.4 = ((f32[2,32,4096]{2,1,0:T(8,128)}), f32[2,32,4096]{2,1,0:T(8,128)S(1)}, u32[]{:S(2)}, u32[]{:S(2)}) async-start(f32[2,32,4096]{2,1,0:T(8,128)} %add_add_fusion), calls=%async_computation.4 | async-start | bytes 2097152 | tf_op jit(solution)/shard_map/all_to_all | solution.py:381
  84.3 1.2 copy-start.7
  102.4 1.3 copy-start.3
  103.7 1.3 copy-start.4
  105.1 1.0 copy-start.1
  125.8 34.2 %all-to-all-start.2 = ((f32[64,64,128]{2,1,0:T(8,128)}), f32[64,64,128]{2,1,0:T(8,128)S(1)}, u32[]{:S(2)}, u32[]{:S(2)}) async-start(f32[64,64,128]{2,1,0:T(8,128)} %bitcast.37), calls=%async_computation.2 | async-start | bytes 4194304 | tf_op jit(solution)/shard_map/all_to_all | solution.py:360
  160.0 1.2 copy-start.2
where the time goes:
time: 170 us; the launch traced here: 169 us
  waiting for transfers between devices  40.1 us (24%)
  blocking collectives  38.7 us (23%)
  Pallas kernels  32.4 us (19%)
  starting transfers between devices  26.8 us (16%)
  local copies, waits for them, and re-layouts  15.4 us (9%)
  other arithmetic  13 us (8%)
  between operations  2.89 us (2%)
    all_to_all x1, waiting for transfers between devices, per_device(): lax.all_to_all(outgoing.reshape(64, 64, 128), 'row', 0, 0, tiled=True)  23.6 us
    all_to_all x1, blocking collectives, over_copies(): return lax.all_to_all(sent, axis, 0, 0, tiled=True).sum(axis=0)  19.7 us
    all_to_all x1, blocking collectives, per_device(): lax.all_to_all(sky_image, 'chan', split_axis=1, concat_axis=0, tiled=True)  19 us
    pallas_call x1, Pallas kernels, per_device(): pl.pallas_call(columns_both, out_shape=(jax.ShapeDtypeStruct((2, *TILES),...  16.8 us
    all_to_all x1, waiting for transfers between devices, per_device(): lax.all_to_all(sent.reshape(64, 64, 128), 'row', 0, 0, tiled=True)  16.1 us
    all_to_all x1, starting transfers between devices, per_device(): lax.all_to_all(sent.reshape(64, 64, 128), 'row', 0, 0, tiled=True)  11.4 us
    unnamed x28, local copies, waits for them, and re-layouts  10.2 us
    pallas_call x1, Pallas kernels, per_device(): pl.pallas_call(rows_back, out_shape=jax.ShapeDtypeStruct(TILES, F32), in_...  8.06 us
  transfers between devices with their start and end apart: 5, of which 3 were waited for; matrix products, arithmetic and copies ran while one was open for 10% of the time, Pallas kernels for 14%

commit v1 on v0

v1 whole, which is shorter than its diff:
```python
import math

import jax
import jax.numpy as jnp
import numpy as np
from jax import lax
from jax.experimental import pallas as pl
from jax.experimental.pallas import tpu as pltpu
from jax.sharding import PartitionSpec as P

data_step = 0.8
primal_step = 0.5
low_taps = (0.0625, 0.25, 0.375, 0.25, 0.0625)
high_taps = (-0.1, -0.3, 0.7, -0.2, -0.1)
low_reverse = (0.0625, 0.25, 0.375, 0.25, 0.0625)
high_reverse = (-0.1, -0.2, 0.7, -0.3, -0.1)

F32 = jnp.float32
SIDE = 4096
RADIX = 32
WIDE = 128


def c_add(a, b):
    re = a[0] + b[0]
    if a[1] is None:
        return (re, b[1])
    return (re, a[1] if b[1] is None else a[1] + b[1])


def c_sub(a, b):
    re = a[0] - b[0]
    if a[1] is None:
        return (re, None if b[1] is None else -b[1])
    return (re, a[1] if b[1] is None else a[1] - b[1])


def c_turn(a, k, n, orient):
    re, im = a
    if k == 0:
        return a
    if 4 * k == n:
        if im is None:
            return (None, re if orient > 0 else -re)
        return (-im, re) if orient > 0 else (im, -re)
    cos, sin = math.cos(2 * math.pi * k / n), orient * math.sin(2 * math.pi * k / n)
    if im is None:
        return (re * cos, re * sin)
    if 8 * k == n:
        return ((re - im) * cos, (re + im) * cos) if orient > 0 else ((re + im) * cos, (im - re) * cos)
    if 8 * k == 3 * n:
        c = -cos
        return ((-re - im) * c, (re - im) * c) if orient > 0 else ((im - re) * c, (-re - im) * c)
    return (re * cos - im * sin, re * sin + im * cos)


def short_fft(items, orient):
    n = len(items)
    if n == 1:
        return list(items)
    even = short_fft(items[0::2], orient)
    odd = short_fft(items[1::2], orient)
    low, high = [], []
    for k in range(n // 2):
        if even[k][1] is None and odd[k][1] is None and 4 * k == n:
            low.append((even[k][0], orient * odd[k][0]))
            high.append((even[k][0], -orient * odd[k][0]))
            continue
        turned = c_turn(odd[k], k, n, orient)
        low.append(c_add(even[k], turned))
        high.append(c_sub(even[k], turned))
    return low + high


def dft_matrix(orient):
    idx = np.arange(WIDE)
    angle = 2 * np.pi * ((idx[:, None] * idx[None, :]) % WIDE) / WIDE
    cos, sin = np.cos(angle) / 64.0, orient * np.sin(angle) / 64.0
    return np.block([[cos, sin], [-sin, cos]])


def halves_first(matrix_rows):
    order = np.arange(WIDE).reshape(64, 2).T.reshape(-1)
    return np.concatenate([matrix_rows[:WIDE][order], matrix_rows[WIDE:][order]])


def high_low(matrix):

    bf = np.asarray(matrix, np.float32).astype(jnp.bfloat16)
    low = (np.asarray(matrix) - bf.astype(np.float64)).astype(jnp.bfloat16)
    return (jnp.asarray(np.stack([bf, low])),)


def twiddle(orient):
    angle = 2 * np.pi * (np.arange(RADIX)[:, None] * np.arange(WIDE)[None, :]) / SIDE
    return jnp.asarray(np.stack([np.cos(angle), orient * np.sin(angle)]), jnp.float32)


def split_two(x):
    high = x.astype(jnp.bfloat16)
    return high, (x - high.astype(jnp.float32)).astype(jnp.bfloat16)


def product(dims, a_pair, b_pair):
    def one(a, b):
        return lax.dot_general(a, b, (dims, ((), ())), preferred_element_type=jnp.float32)

    return one(a_pair[0], b_pair[0]) + (one(a_pair[1], b_pair[0]) + one(a_pair[0], b_pair[1]))


def spread(matrix_ref, block):
    return product(((1,), (1,)), (matrix_ref[0], matrix_ref[1]), split_two(block))


def gather(block, matrix_ref):
    return product(((0,), (0,)), split_two(block), (matrix_ref[0], matrix_ref[1]))


def c_mul(a, b_re, b_im):
    return (a[0] * b_re - a[1] * b_im, a[0] * b_im + a[1] * b_re)


MESH = pl.DeviceIdType.MESH
PEERS = 64
CHUNK = 64
PIECE = 16
PIECES = 4
PRIOR_AFTER = 1


def chunk_row(g, c, a_hi, e):
    return g * PIECE + c * 8 + a_hi * 2 + e


def step(
    radius_ref, x_hbm, dual_hbm, vis_hbm, weight_hbm, prior_hbm, limit_hbm, tw_ref, sr_ref, gc_ref, sc_ref, gr_ref,
    image_ref, fourier_ref, wavelet_ref,
    x_ref, dual_ref, vis_ref, weight_ref, prior_ref, limit_ref,
    sent, arrived, sent_back, returned, held, wide, sums, own_sums, all_sums,
    near_send, far_send, sky_got, near_got, far_got, grown, edge_send, prior_got, edge_got, spread_new,
    load_sem, own_sem, send_sem, recv_sem, back_send, back_recv, sum_send, sum_recv, sky_send, sky_recv, pri_send, pri_recv,
):
    r, ch = lax.axis_index("row"), lax.axis_index("chan")
    other = 1 - ch
    after, before = lax.rem(r + 1, PEERS), lax.rem(r + PEERS - 1, PEERS)

    loads = [
        pltpu.make_async_copy(src, dst, load_sem.at[i])
        for i, (src, dst) in enumerate(
            (
                (x_hbm, x_ref), (prior_hbm, prior_ref), (limit_hbm, limit_ref),
                (dual_hbm, dual_ref), (vis_hbm, vis_ref), (weight_hbm, weight_ref),
            )
        )
    ]
    for load in loads:
        load.start()

    barrier = pltpu.get_barrier_semaphore()

    def greet(i, _):
        pl.semaphore_signal(barrier, inc=1, device_id=(lax.rem(r + i, PEERS), ch), device_id_type=MESH)
        return 0

    lax.fori_loop(1, PEERS, greet, 0)
    for row in (r, after, before):
        pl.semaphore_signal(barrier, inc=1, device_id=(row, other), device_id_type=MESH)

    def remote(src, dst, send, recv, row, chan):
        return pltpu.make_async_remote_copy(
            src_ref=src, dst_ref=dst, send_sem=send, recv_sem=recv, device_id=(row, chan), device_id_type=MESH
        )

    loads[0].wait()

    def row_short(at, _):
        items = [(x_ref[at, p], None) for p in range(RADIX)]
        done = short_fft(items, -1)
        a_hi, a_mid = at // 2, at % 2
        for q in range(RADIX):
            value = done[q]
            if value[1] is None:
                re = value[0] * tw_ref[0, pl.ds(q, 1), :]
                im = value[0] * tw_ref[1, pl.ds(q, 1), :]
            else:
                re, im = c_mul(value, tw_ref[0, pl.ds(q, 1), :], tw_ref[1, pl.ds(q, 1), :])
            row = pl.ds(pl.multiple_of((q % 8) * 16 + a_mid * 8, 8), 8)
            held[(q // 8) * 4 + a_hi, row, 0:WIDE] = re
            held[(q // 8) * 4 + a_hi, row, WIDE:] = im
        return 0

    lax.fori_loop(0, 8, row_short, 0)

    first_here = ch == 0

    def edges(t, _):
        low, high = x_ref[4, t][0:2], x_ref[3, t][6:8]
        near_send[t] = jnp.where(first_here, high, low)
        far_send[0, t] = x_ref[7, t][6:8]
        far_send[1, t] = x_ref[0, t][0:2]
        return 0

    lax.fori_loop(0, 32, edges, 0)
    pl.semaphore_wait(barrier, PEERS + 2)

    half = pl.ds(pl.multiple_of(other * 4, 4), 4)
    sky_copies = [
        remote(x_ref.at[half], sky_got, sky_send.at[0], sky_recv.at[0], r, other),
        remote(near_send, near_got, sky_send.at[1], sky_recv.at[1], r, other),
    ]
    for copy in sky_copies:
        copy.start()
    far_up = remote(far_send.at[0], far_got.at[ch], sky_send.at[2], sky_recv.at[2 + ch], after, 0)
    far_down = remote(far_send.at[1], far_got.at[ch], sky_send.at[3], sky_recv.at[2 + ch], before, 1)
    far_up.start()
    far_down.start()

    def piece_copies(src, dst, send, recv, g):
        def one(i, _):
            d = lax.rem(r + i, PEERS)
            take = pl.ds(pl.multiple_of(d * CHUNK + g * PIECE, PIECE), PIECE)
            give = pl.ds(pl.multiple_of(r * CHUNK + g * PIECE, PIECE), PIECE)
            remote(src.at[take], dst.at[give], send.at[g], recv.at[g], d, ch).start()
            return 0

        lax.fori_loop(1, PEERS, one, 0)
        mine = pl.ds(pl.multiple_of(r * CHUNK + g * PIECE, PIECE), PIECE)
        return pltpu.make_async_copy(src.at[mine], dst.at[mine], own_sem)

    def all_of(src, dst, send, recv, g):
        rows = pl.ds(0, (PEERS - 1) * PIECE)
        return remote(src.at[rows], dst.at[rows], send.at[g], recv.at[g], after, ch)

    def row_piece(g, _):
        def block(a_hi, _):
            result = spread(sr_ref, held[g * 4 + a_hi])
            for c in range(2):
                for e in range(2):
                    for d in range(0, 64, 8):
                        m = c * 128 + e * 64 + d
                        sent[pl.ds(d * CHUNK + chunk_row(g, c, a_hi, e), 8, stride=CHUNK), :] = result[m : m + 8]
            return 0

        lax.fori_loop(0, 4, block, 0)
        own = piece_copies(sent, arrived, send_sem, recv_sem, g)
        own.start()
        own.wait()
        return 0

    lax.fori_loop(0, PIECES, row_piece, 0)

    for load in loads[3:]:
        load.wait()
    sums[...] = jnp.zeros_like(sums)

    def column_piece(g, _):
        all_of(sent, arrived, send_sem, recv_sem, g).wait_recv()

        def block(i, _):
            l_hi, e = i // 2, i % 2
            rows = []
            for c in range(2):
                for jh in range(2):
                    rows.append(arrived[pl.ds(chunk_row(g, c, jh * 2 + l_hi, e), PEERS, stride=CHUNK), :])
            result = gather(jnp.concatenate(rows), gc_ref)
            for q_lo in range(8):
                row = pl.ds(pl.multiple_of(((e * 4 + g) * 8 + q_lo) * 32 + l_hi * 16, 16), 16)
                wide[0, row, :] = result[q_lo * 16 : q_lo * 16 + 16, 0:WIDE]
                wide[1, row, :] = result[q_lo * 16 : q_lo * 16 + 16, WIDE:]
            return 0

        lax.fori_loop(0, 4, block, 0)

        def short(e, _):
            q_hi = e * 4 + g
            items = []
            for l in range(RADIX):
                row = pl.ds(q_hi * 256 + l, 8, stride=32)
                items.append(
                    c_mul((wide[0, row, :], wide[1, row, :]), tw_ref[0, pl.ds(l, 1), :], tw_ref[1, pl.ds(l, 1), :])
                )
            freq = short_fft(items, -1)
            total, total_vis = sums[0], sums[1]
            items = []
            for v in range(RADIX):
                weight = weight_ref[q_hi, v]
                vis_re, vis_im = vis_ref[0, q_hi, v], vis_ref[1, q_hi, v]
                re = dual_ref[0, q_hi, v] * (1.0 / data_step) + weight * freq[v][0] - vis_re
                im = dual_ref[1, q_hi, v] * (1.0 / data_step) + weight * freq[v][1] - vis_im
                total = total + (re * re + im * im)
                total_vis = total_vis + (vis_re * vis_re + vis_im * vis_im)
                fourier_ref[0, q_hi, v] = re
                fourier_ref[1, q_hi, v] = im
                items.append((weight * re, weight * im))
            sums[0] = total
            sums[1] = total_vis
            done = short_fft(items, 1)
            for l in range(RADIX):
                re, im = c_mul(done[l], tw_ref[0, pl.ds(l, 1), :], -tw_ref[1, pl.ds(l, 1), :])
                row = pl.ds((l % 16) * 8, 8)
                held[(l // 16) * 8 + q_hi, row, 0:WIDE] = re
                held[(l // 16) * 8 + q_hi, row, WIDE:] = im
            return 0

        lax.fori_loop(0, 2, short, 0)

        def block_back(i, _):
            l_hi, e = i // 2, i % 2
            result = spread(sc_ref, held[l_hi * 8 + e * 4 + g])
            for c in range(2):
                for jh in range(2):
                    for s in range(0, 64, 8):
                        m = c * 128 + jh * 64 + s
                        start = s * CHUNK + chunk_row(g, c, jh * 2 + l_hi, e)
                        sent_back[pl.ds(start, 8, stride=CHUNK), :] = result[m : m + 8]
            return 0

        lax.fori_loop(0, 4, block_back, 0)
        own = piece_copies(sent_back, returned, back_send, back_recv, g)
        own.start()
        own.wait()
        return 0

    lane = lax.broadcasted_iota(jnp.int32, (8, 128), 1)

    def filter_column(load, low_set, high_set, carry):
        taps = [load(p) for p in range(5)]
        low = taps[0] * low_set[0]
        high = taps[0] * high_set[0]
        for p in range(1, 5):
            low = low + taps[p] * low_set[p]
            high = high + taps[p] * high_set[p]
        return finish_column(low, high, low_set, high_set, carry)

    def finish_column(low, high, low_set, high_set, carry):
        old0, old1, unfinished = carry
        terms = [high * low_set[p] + low * high_set[p] for p in range(5)]
        new0 = pltpu.roll(terms[0], 2, 1)
        new1 = pltpu.roll(terms[1], 1, 1)
        new3 = pltpu.roll(terms[3], 127, 1)
        new4 = pltpu.roll(terms[4], 126, 1)
        finished = unfinished + jnp.where(lane >= 127, new3, 0.0) + jnp.where(lane >= 126, new4, 0.0)
        started = (
            terms[2]
            + (jnp.where(lane >= 2, new0, old0) + jnp.where(lane >= 1, new1, old1))
            + (jnp.where(lane < 127, new3, 0.0) + jnp.where(lane < 126, new4, 0.0))
        )
        return finished, (new0, new1, started)

    zero = jnp.zeros((8, 128), F32)
    prior_copies = [
        remote(wavelet_ref.at[other], prior_got, pri_send.at[0], pri_recv.at[0], r, other)
    ] + [
        remote(
            edge_send.at[c], edge_got.at[1 - ch], pri_send.at[1 + c], pri_recv.at[2 - ch],
            lax.rem(r + PEERS - 1 + 2 * ch, PEERS), c,
        )
        for c in range(2)
    ]

    def prior_step():
        for load in loads[1:3]:
            load.wait()
        for copy in sky_copies:
            copy.wait_recv()
        for k in range(2):
            remote(far_send.at[0], far_got.at[k], sky_send.at[2], sky_recv.at[2 + k], r, other).wait_recv()
        no_far = jnp.logical_or(
            jnp.logical_and(ch == 0, r == 0), jnp.logical_and(ch == 1, r == PEERS - 1)
        )

        def grow(t, _):
            for k in range(4):
                grown[ch, t, 8 + 8 * k : 16 + 8 * k, :] = x_ref[ch * 4 + k, t]
                grown[other, t, 8 + 8 * k : 16 + 8 * k, :] = sky_got[k, t]
            near_own = jnp.where(first_here, x_ref[4, t][0:2], x_ref[3, t][6:8])
            near_other = near_got[t]
            far_own = jnp.where(no_far, 0.0, far_got[ch, t])
            far_other = jnp.where(no_far, 0.0, far_got[other, t])
            grown[ch, t, 6:8, :] = jnp.where(first_here, far_own, near_own)
            grown[ch, t, 40:42, :] = jnp.where(first_here, near_own, far_own)
            grown[other, t, 6:8, :] = jnp.where(first_here, far_other, near_other)
            grown[other, t, 40:42, :] = jnp.where(first_here, near_other, far_other)
            return 0

        lax.fori_loop(0, 32, grow, 0)

        def close(t, filtered):
            for k in range(4):
                s0 = prior_ref[0, k, t] + filtered[0][k]
                s1 = prior_ref[1, k, t] + filtered[1][k]
                limit = limit_ref[k, t]
                scale = limit / jnp.maximum(jnp.sqrt(s0 * s0 + s1 * s1), limit)
                wavelet_ref[0, k, t] = s0 * scale
                wavelet_ref[1, k, t] = s1 * scale

        def columns(t, carry):
            filtered, new = [[], []], []
            for c in range(2):
                for k in range(4):
                    finished, kept = filter_column(
                        lambda p: grown[c, t, 6 + 8 * k + p : 14 + 8 * k + p, :], low_taps, high_taps, carry[c * 4 + k]
                    )
                    filtered[c].append(finished)
                    new.append(kept)
            close(jnp.maximum(t - 1, 0), filtered)
            return tuple(new)

        carry = lax.fori_loop(0, 32, columns, ((zero, zero, zero),) * 8)
        close(31, [[carry[c * 4 + k][2] for k in range(4)] for c in range(2)])

        def edge(t, _):
            for c in range(2):
                edge_send[c, t] = jnp.where(
                    first_here, wavelet_ref[c, 0, t][0:2], wavelet_ref[c, 3, t][6:8]
                )
            return 0

        lax.fori_loop(0, 32, edge, 0)

        for copy in prior_copies:
            copy.start()


    def adjoint_step():
        prior_copies[0].wait_recv()
        for k in range(2):
            remote(edge_send.at[0], edge_got.at[k], pri_send.at[1], pri_recv.at[1 + k], r, other).wait_recv()

        def fill(t, _):
            for k in range(4):
                mine = pl.ds(pl.multiple_of(8 + ch * 32 + 8 * k, 8), 8)
                theirs = pl.ds(pl.multiple_of(8 + other * 32 + 8 * k, 8), 8)
                spread_new[t, mine, :] = wavelet_ref[ch, k, t]
                spread_new[t, theirs, :] = prior_got[k, t]
            spread_new[t, 6:8, :] = jnp.where(r == 0, 0.0, edge_got[0, t])
            spread_new[t, 72:74, :] = jnp.where(r == PEERS - 1, 0.0, edge_got[1, t])
            return 0

        lax.fori_loop(0, 32, fill, 0)

        def close(t, k, filtered):
            image_ref[k, t] = x_ref[k, t] - primal_step * filtered

        def columns(t, carry):
            new = []
            for k in range(8):
                finished, kept = filter_column(
                    lambda p: spread_new[t, 6 + 8 * k + p : 14 + 8 * k + p, :], low_reverse, high_reverse, carry[k]
                )
                close(jnp.maximum(t - 1, 0), k, finished)
                new.append(kept)
            return tuple(new)

        carry = lax.fori_loop(0, 32, columns, ((zero, zero, zero),) * 8)
        for k in range(8):
            close(31, k, carry[k][2])

    lax.fori_loop(0, PRIOR_AFTER, column_piece, 0)
    prior_step()
    lax.fori_loop(PRIOR_AFTER, PIECES, column_piece, 0)

    own_sums[0:1] = jnp.sum(sums[0], axis=0, keepdims=True)
    own_sums[1:2] = jnp.sum(sums[1], axis=0, keepdims=True)
    all_sums[r] = own_sums[...]

    def tell(i, _):
        remote(own_sums, all_sums.at[r], sum_send, sum_recv, lax.rem(r + i, PEERS), ch).start()
        return 0

    lax.fori_loop(1, PEERS, tell, 0)
    adjoint_step()
    every = pl.ds(0, PEERS - 1)
    told = remote(all_sums.at[every], all_sums.at[every], sum_send, sum_recv, after, ch)
    told.wait_recv()
    norms = jnp.sum(all_sums[...], axis=0)
    resid_norm = jnp.sum(norms[0:1], axis=1, keepdims=True)
    data_norm = jnp.sum(norms[1:2], axis=1, keepdims=True)
    shrink = data_step * (1.0 - radius_ref[0] * jnp.sqrt(data_norm) / jnp.sqrt(resid_norm))
    shrink = jnp.broadcast_to(shrink, (8, 128))

    def scale(i, _):
        for v in range(32):
            for part in range(2):
                fourier_ref[part, i, v] = fourier_ref[part, i, v] * shrink
        return 0

    lax.fori_loop(0, 8, scale, 0)

    def back_piece(g, _):
        all_of(sent_back, returned, back_send, back_recv, g).wait_recv()

        def block(a_hi, _):
            rows = []
            for c in range(2):
                for e in range(2):
                    rows.append(returned[pl.ds(chunk_row(g, c, a_hi, e), PEERS, stride=CHUNK), :])
            result = gather(jnp.concatenate(rows), gr_ref)
            for a_lo in range(16):
                row = pl.ds(pl.multiple_of((a_hi * 16 + a_lo) * 32 + g * 8, 8), 8)
                wide[0, row, :] = result[a_lo * 8 : a_lo * 8 + 8, 0:WIDE]
                wide[1, row, :] = result[a_lo * 8 : a_lo * 8 + 8, WIDE:]
            return 0

        lax.fori_loop(0, 4, block, 0)
        return 0

    lax.fori_loop(0, PIECES, back_piece, 0)

    def finish(at, _):
        items = []
        for q in range(RADIX):
            row = pl.ds(at * 256 + q, 8, stride=32)
            items.append(
                c_mul((wide[0, row, :], wide[1, row, :]), tw_ref[0, pl.ds(q, 1), :], -tw_ref[1, pl.ds(q, 1), :])
            )
        done = short_fft(items, 1)
        factor = shrink * primal_step
        for p in range(RADIX):
            image_ref[at, p] = jnp.maximum(image_ref[at, p] - done[p][0] * factor, 0.0)
        return 0

    lax.fori_loop(0, 8, finish, 0)

    for copy in sky_copies + [far_up, far_down] + prior_copies + [told]:
        copy.wait_send()

    def drain(g, _):
        all_of(sent, arrived, send_sem, recv_sem, g).wait_send()
        all_of(sent_back, returned, back_send, back_recv, g).wait_send()
        return 0

    lax.fori_loop(0, PIECES, drain, 0)


def tiles(array):
    lead, n = array.shape[:-2], array.ndim - 2
    array = array.reshape(lead + (array.shape[-2] // 8, 8, 32, 128))
    return array.transpose(tuple(range(n)) + (n, n + 2, n + 1, n + 3))


def untiles(array):
    n = array.ndim - 4
    rows = array.shape[n] * 8
    array = array.transpose(tuple(range(n)) + (n, n + 2, n + 1, n + 3))
    return array.reshape(array.shape[:n] + (rows, SIDE))


def per_device(sky_image, fourier_dual, visibilities, weights, radius, wavelet_dual, reweight):
    forward, backward = dft_matrix(-1.0), dft_matrix(1.0)
    tables = (
        twiddle(-1.0),
        high_low(halves_first(forward.T))[0],
        high_low(halves_first(forward))[0],
        high_low(halves_first(backward.T))[0],
        high_low(halves_first(backward))[0],
    )
    vmem, dma = pltpu.VMEM, pltpu.SemaphoreType.DMA
    in_vmem, in_any = pl.BlockSpec(memory_space=pltpu.VMEM), pl.BlockSpec(memory_space=pl.ANY)
    image, fourier_new, wavelet_new = pl.pallas_call(
        step,
        out_shape=(
            jax.ShapeDtypeStruct((8, 32, 8, 128), F32),
            jax.ShapeDtypeStruct((2, 8, 32, 8, 128), F32),
            jax.ShapeDtypeStruct((2, 4, 32, 8, 128), F32),
        ),
        in_specs=[pl.BlockSpec(memory_space=pltpu.SMEM)] + [in_any] * 6 + [in_vmem] * 5,
        out_specs=(in_vmem,) * 3,
        scratch_shapes=[
            vmem((8, 32, 8, 128), F32), vmem((2, 8, 32, 8, 128), F32), vmem((2, 8, 32, 8, 128), F32),
            vmem((8, 32, 8, 128), F32), vmem((2, 4, 32, 8, 128), F32), vmem((4, 32, 8, 128), F32),
            vmem((4096, 128), F32), vmem((4096, 128), F32), vmem((4096, 128), F32), vmem((4096, 128), F32),
            vmem((16, 128, 256), F32), vmem((2, 2048, 128), F32),
            vmem((2, 8, 128), F32), vmem((2, 128), F32), vmem((PEERS, 2, 128), F32),
            vmem((32, 2, 128), F32), vmem((2, 32, 2, 128), F32),
            vmem((4, 32, 8, 128), F32), vmem((32, 2, 128), F32), vmem((2, 32, 2, 128), F32),
            vmem((2, 32, 48, 128), F32),
            vmem((2, 32, 2, 128), F32), vmem((4, 32, 8, 128), F32), vmem((2, 32, 2, 128), F32),
            vmem((32, 80, 128), F32),
            dma((6,)), dma, dma((PIECES,)), dma((PIECES,)), dma((PIECES,)), dma((PIECES,)),
            dma, dma, dma((4,)), dma((4,)), dma((3,)), dma((3,)),
        ],
        compiler_params=pltpu.CompilerParams(
            collective_id=0, has_side_effects=True, vmem_limit_bytes=60 << 20
        ),
    )(
        radius, tiles(sky_image[0]), tiles(fourier_dual[:, 0]), tiles(visibilities[:, 0]), tiles(weights[0]),
        tiles(wavelet_dual), tiles(reweight), *tables,
    )
    return (untiles(image)[None], untiles(fourier_new)[:, None], untiles(wavelet_new))


def solution(mesh):
    in_specs = (
        P("chan", "row", None),
        P(None, "chan", "row", None),
        P(None, "chan", "row", None),
        P("chan", "row", None),
        P("chan"),
        P(None, ("row", "chan"), None),
        P(("row", "chan"), None),
    )
    out_specs = (
        P("chan", "row", None),
        P(None, "chan", "row", None),
        P(None, ("row", "chan"), None),
    )
    return jax.shard_map(
        per_device, mesh=mesh, in_specs=in_specs, out_specs=out_specs, check_vma=False
    )
```

time: 170 us -> 104 us (0.61)
  Pallas kernels: 32.4 us -> 97.3 us
  waiting for transfers between devices: 40.1 us -> 0 us
  blocking collectives: 38.7 us -> 0 us
  starting transfers between devices: 26.8 us -> 0 us
  other arithmetic: 13 us -> 0 us
  local copies, waits for them, and re-layouts: 15.4 us -> 5.35 us
    pallas_call x3 -> x1, Pallas kernels: 32.4 us -> 97.3 us  [per_device(): pl.pallas_call(step, out_shape=(jax.ShapeDtypeStruct((8, 32, 8, 128), F32...]
    all_to_all x3 -> x0, waiting for transfers between devices: 39.7 us -> none  [the longest x1 23.6 us: per_device(): lax.all_to_all(outgoing.reshape(64, 64, 128), 'row', 0, 0, tiled=True)]
    all_to_all x2 -> x0, blocking collectives: 38.7 us -> none  [the longest x1 19.7 us: over_copies(): return lax.all_to_all(sent, axis, 0, 0, tiled=True).sum(axis=0)]
    all_to_all x3 -> x0, starting transfers between devices: 19.7 us -> none  [the longest x1 11.4 us: per_device(): lax.all_to_all(sent.reshape(64, 64, 128), 'row', 0, 0, tiled=True)]
    ppermute x2 -> x0, starting transfers between devices: 7.05 us -> none  [the longest x1 4.87 us: extended_2(): lax.ppermute(first, axis, [(b, a) for a, b in up])]
    add x5 -> x0, other arithmetic: 5.79 us -> none  [the longest x1 3.2 us: analysis(): filter_columns(filter_rows(extended, high_set), low_set)]
    unnamed x28 -> x7, local copies, waits for them, and re-layouts: 10.2 us -> 5.35 us
    another operation x1 -> x0, other arithmetic: 3.11 us -> none  [per_device(): fourier_new = untiles(resid * shrink[0])[:, None]]
  transfers between devices with their start and end apart: 5 -> 0, of which waited for: 3 -> 0; matrix products, arithmetic and copies ran while one was open for 10% -> 0% of each run, Pallas kernels for 14% -> 0%
where the time goes in v1:
time: 104 us
  Pallas kernels  97.3 us (94%)
  local copies, waits for them, and re-layouts  5.35 us (5%)
  between operations  1.3 us (1%)
    pallas_call x1, Pallas kernels, per_device(): pl.pallas_call(step, out_shape=(jax.ShapeDtypeStruct((8, 32, 8, 128), F32...  97.3 us
    unnamed x7, local copies, waits for them, and re-layouts  5.35 us

profile of v1, /device:TPU:1, one launch (start us, length us, event | category | flops | bytes accessed | tf_op | source)
XLA Modules:
  0.0 104.0 jit_solution(15563255192637908158)
XLA Ops:
  1.3 97.3 %shard_map.139 = (f32[8,32,8,128]{3,2,1,0:T(8,128)}, f32[2,8,32,8,128]{4,3,2,1,0:T(8,128)}, f32[2,4,32,8,128]{4,3,2,1,0:T(8,128)}) custom-call(f32[1]{0:T(128)S(6)} %copy.18.radius_ref, f32[8,32,8,128]{3,2,1,0:T(8,128)} %bitcast.30, f32[2,8,32,8,128]{4,3,2,1,0:T(8,128)} %bitcast.27, f32[2,8,32,8,128]{4,3,2,1,0:T(8,128)} %bitcast.28, ...), custom_call_target="tpu_custom_call" | custom-call | tf_op jit(solution)/shard_map/pallas_call | solution.py:560
  98.6 0.0 copy-start
  98.6 2.4 %copy.19 = f32[1,64,4096]{2,1,0:T(8,128)} copy(f32[1,64,4096]{2,1,0:T(8,128)} %bitcast.34) | data formatting | bytes 2097152
  101.1 0.0 copy-done
  101.1 0.0 copy-start.1
  101.1 1.3 %copy.20 = f32[2,1,64,4096]{3,2,1,0:T(8,128)} copy(f32[2,1,64,4096]{3,2,1,0:T(8,128)S(1)} %bitcast.29) | data formatting | bytes 4194304
  102.4 0.6 copy-done.1
  103.0 1.0 copy.21
Async XLA Ops:
  98.6 2.4 %copy-start = (f32[2,8,32,8,128]{4,3,2,1,0:T(8,128)S(1)}, f32[2,8,32,8,128]{4,3,2,1,0:T(8,128)}, u32[]{:S(2)}) copy-start(f32[2,8,32,8,128]{4,3,2,1,0:T(8,128)} %get-tuple-element.7) | copy-start | bytes 6291460
  101.1 2.0 %copy-start.1 = (f32[2,4,32,8,128]{4,3,2,1,0:T(8,128)S(1)}, f32[2,4,32,8,128]{4,3,2,1,0:T(8,128)}, u32[]{:S(2)}) copy-start(f32[2,4,32,8,128]{4,3,2,1,0:T(8,128)} %get-tuple-element.8) | copy-start | bytes 3145732

commit v2 on v1

--- a/solution.py
+++ b/solution.py
@@ -125,18 +125,18 @@
 CHUNK = 64
 PIECE = 16
 PIECES = 4
-PRIOR_AFTER = 1
+VMEM_MIB = 40
 
 
 def chunk_row(g, c, a_hi, e):
-    return g * PIECE + c * 8 + a_hi * 2 + e
+    return g * PIECE + (a_hi // 2) * 8 + c * 4 + (a_hi % 2) * 2 + e
 
 
 def step(
-    radius_ref, x_hbm, dual_hbm, vis_hbm, weight_hbm, prior_hbm, limit_hbm, tw_ref, sr_ref, gc_ref, sc_ref, gr_ref,
+    radius_ref, x_hbm, prior_hbm, limit_hbm, dual_hbm, vis_hbm, weight_hbm, tw_hbm, rows_hbm, columns_hbm,
     image_ref, fourier_ref, wavelet_ref,
-    x_ref, dual_ref, vis_ref, weight_ref, prior_ref, limit_ref,
-    sent, arrived, sent_back, returned, held, wide, sums, own_sums, all_sums,
+    x_ref, dual_ref, vis_ref, weight_ref, prior_ref, limit_ref, tw_ref, rows_ref, columns_ref,
+    sent, arrived, sent_back, returned, held, facet_held, facet_sent, wide, sums, own_sums, all_sums,
     near_send, far_send, sky_got, near_got, far_got, grown, edge_send, prior_got, edge_got, spread_new,
     load_sem, own_sem, send_sem, recv_sem, back_send, back_recv, sum_send, sum_recv, sky_send, sky_recv, pri_send, pri_recv,
 ):
@@ -148,7 +148,8 @@
         pltpu.make_async_copy(src, dst, load_sem.at[i])
         for i, (src, dst) in enumerate(
             (
-                (x_hbm, x_ref), (prior_hbm, prior_ref), (limit_hbm, limit_ref),
+                (x_hbm, x_ref), (tw_hbm, tw_ref), (rows_hbm, rows_ref), (columns_hbm, columns_ref),
+                (prior_hbm, prior_ref), (limit_hbm, limit_ref),
                 (dual_hbm, dual_ref), (vis_hbm, vis_ref), (weight_hbm, weight_ref),
             )
         )
@@ -158,13 +159,16 @@
 
     barrier = pltpu.get_barrier_semaphore()
 
+    def greet_other(i, _):
+        pl.semaphore_signal(barrier, inc=1, device_id=(lax.rem(r + i, PEERS), other), device_id_type=MESH)
+        return 0
+
     def greet(i, _):
         pl.semaphore_signal(barrier, inc=1, device_id=(lax.rem(r + i, PEERS), ch), device_id_type=MESH)
         return 0
 
     lax.fori_loop(1, PEERS, greet, 0)
-    for row in (r, after, before):
-        pl.semaphore_signal(barrier, inc=1, device_id=(row, other), device_id_type=MESH)
+    lax.fori_loop(0, PEERS, greet_other, 0)
 
     def remote(src, dst, send, recv, row, chan):
         return pltpu.make_async_remote_copy(
@@ -172,10 +176,9 @@
         )
 
     loads[0].wait()
-
-    def row_short(at, _):
-        items = [(x_ref[at, p], None) for p in range(RADIX)]
-        done = short_fft(items, -1)
+    loads[1].wait()
+
+    def turn_rows(done, into, blocks, at):
         a_hi, a_mid = at // 2, at % 2
         for q in range(RADIX):
             value = done[q]
@@ -185,8 +188,18 @@
             else:
                 re, im = c_mul(value, tw_ref[0, pl.ds(q, 1), :], tw_ref[1, pl.ds(q, 1), :])
             row = pl.ds(pl.multiple_of((q % 8) * 16 + a_mid * 8, 8), 8)
-            held[(q // 8) * 4 + a_hi, row, 0:WIDE] = re
-            held[(q // 8) * 4 + a_hi, row, WIDE:] = im
+            into[(q // 8) * blocks + a_hi, row, 0:WIDE] = re
+            into[(q // 8) * blocks + a_hi, row, WIDE:] = im
+
+    side, z, low = (r // 8) % 2, r // 16, r % 8
+
+    def peer(i, its_side):
+        return lax.rem(z + i // 8, 4) * 16 + its_side * 8 + lax.rem(low + i % 8, 8)
+
+    def row_short(at, _):
+        items = [(x_ref[at, p], None) for p in range(RADIX)]
+        done = short_fft(items, -1)
+        turn_rows(done, held, 4, at)
         return 0
 
     lax.fori_loop(0, 8, row_short, 0)
@@ -201,7 +214,7 @@
         return 0
 
     lax.fori_loop(0, 32, edges, 0)
-    pl.semaphore_wait(barrier, PEERS + 2)
+    pl.semaphore_wait(barrier, 2 * PEERS - 1)
 
     half = pl.ds(pl.multiple_of(other * 4, 4), 4)
     sky_copies = [
@@ -215,17 +228,16 @@
     far_up.start()
     far_down.start()
 
-    def piece_copies(src, dst, send, recv, g):
+    loads[2].wait()
+    def back_copies(g, its_side, first):
         def one(i, _):
-            d = lax.rem(r + i, PEERS)
+            d = peer(i, its_side)
             take = pl.ds(pl.multiple_of(d * CHUNK + g * PIECE, PIECE), PIECE)
             give = pl.ds(pl.multiple_of(r * CHUNK + g * PIECE, PIECE), PIECE)
-            remote(src.at[take], dst.at[give], send.at[g], recv.at[g], d, ch).start()
-            return 0
-
-        lax.fori_loop(1, PEERS, one, 0)
-        mine = pl.ds(pl.multiple_of(r * CHUNK + g * PIECE, PIECE), PIECE)
-        return pltpu.make_async_copy(src.at[mine], dst.at[mine], own_sem)
+            remote(sent_back.at[take], returned.at[give], back_send.at[g], back_recv.at[g], d, ch).start()
+            return 0
+
+        lax.fori_loop(first, PEERS // 2, one, 0)
 
     def all_of(src, dst, send, recv, g):
         rows = pl.ds(0, (PEERS - 1) * PIECE)
@@ -233,7 +245,7 @@
 
     def row_piece(g, _):
         def block(a_hi, _):
-            result = spread(sr_ref, held[g * 4 + a_hi])
+            result = spread(rows_ref, held[g * 4 + a_hi])
             for c in range(2):
                 for e in range(2):
                     for d in range(0, 64, 8):
@@ -241,35 +253,87 @@
                         sent[pl.ds(d * CHUNK + chunk_row(g, c, a_hi, e), 8, stride=CHUNK), :] = result[m : m + 8]
             return 0
 
-        lax.fori_loop(0, 4, block, 0)
-        own = piece_copies(sent, arrived, send_sem, recv_sem, g)
+        lax.fori_loop(0, 4, block, 0, unroll=True)
+
+        def one(i, _):
+            d = peer(i, side)
+            take = pl.ds(pl.multiple_of(d * CHUNK + g * PIECE, PIECE), PIECE)
+            give = pl.ds(pl.multiple_of(r * CHUNK + g * PIECE, PIECE), PIECE)
+            remote(sent.at[take], arrived.at[give], send_sem.at[g], recv_sem.at[g], d, ch).start()
+            return 0
+
+        lax.fori_loop(1, PEERS // 2, one, 0)
+        mine = pl.ds(pl.multiple_of(r * CHUNK + g * PIECE, PIECE), PIECE)
+        own = pltpu.make_async_copy(sent.at[mine], arrived.at[mine], own_sem)
         own.start()
         own.wait()
         return 0
 
     lax.fori_loop(0, PIECES, row_piece, 0)
 
-    for load in loads[3:]:
+    for copy in sky_copies:
+        copy.wait_recv()
+
+    def facet_short(at, _):
+        done = short_fft([(sky_got[at, p], None) for p in range(RADIX)], -1)
+        turn_rows(done, facet_held, 2, at)
+        return 0
+
+    lax.fori_loop(0, 4, facet_short, 0)
+
+    def facet_piece(g, _):
+        def own_half(i, _):
+            d = peer(i, 1 - side)
+            take = pl.ds(pl.multiple_of(d * CHUNK + g * PIECE + ch * 8, 8), 8)
+            give = pl.ds(pl.multiple_of(r * CHUNK + g * PIECE + ch * 8, 8), 8)
+            remote(sent.at[take], arrived.at[give], send_sem.at[g], recv_sem.at[g], d, ch).start()
+            return 0
+
+        lax.fori_loop(0, PEERS // 2, own_half, 0)
+
+        def block(l_hi, _):
+            result = spread(rows_ref, facet_held[g * 2 + l_hi])
+            for c in range(2):
+                for e in range(2):
+                    for d in range(0, 64, 8):
+                        m = c * 128 + e * 64 + d
+                        start = d * 32 + g * 8 + c * 4 + l_hi * 2 + e
+                        facet_sent[pl.ds(start, 8, stride=32), :] = result[m : m + 8]
+            return 0
+
+        lax.fori_loop(0, 2, block, 0, unroll=True)
+
+        def other_half(i, _):
+            d = peer(i, 1 - side)
+            take = pl.ds(pl.multiple_of(d * 32 + g * 8, 8), 8)
+            give = pl.ds(pl.multiple_of(r * CHUNK + g * PIECE + ch * 8, 8), 8)
+            remote(facet_sent.at[take], arrived.at[give], send_sem.at[g], recv_sem.at[g], d, other).start()
+            return 0
+
+        lax.fori_loop(0, PEERS // 2, other_half, 0)
+        return 0
+
+    lax.fori_loop(0, PIECES, facet_piece, 0)
+
+    for load in loads[3:4] + loads[6:]:
         load.wait()
     sums[...] = jnp.zeros_like(sums)
 
     def column_piece(g, _):
-        all_of(sent, arrived, send_sem, recv_sem, g).wait_recv()
-
         def block(i, _):
             l_hi, e = i // 2, i % 2
             rows = []
             for c in range(2):
                 for jh in range(2):
                     rows.append(arrived[pl.ds(chunk_row(g, c, jh * 2 + l_hi, e), PEERS, stride=CHUNK), :])
-            result = gather(jnp.concatenate(rows), gc_ref)
+            result = gather(jnp.concatenate(rows), columns_ref)
             for q_lo in range(8):
                 row = pl.ds(pl.multiple_of(((e * 4 + g) * 8 + q_lo) * 32 + l_hi * 16, 16), 16)
                 wide[0, row, :] = result[q_lo * 16 : q_lo * 16 + 16, 0:WIDE]
                 wide[1, row, :] = result[q_lo * 16 : q_lo * 16 + 16, WIDE:]
             return 0
 
-        lax.fori_loop(0, 4, block, 0)
+        lax.fori_loop(0, 4, block, 0, unroll=True)
 
         def short(e, _):
             q_hi = e * 4 + g
@@ -306,7 +370,7 @@
 
         def block_back(i, _):
             l_hi, e = i // 2, i % 2
-            result = spread(sc_ref, held[l_hi * 8 + e * 4 + g])
+            result = spread(columns_ref, held[l_hi * 8 + e * 4 + g])
             for c in range(2):
                 for jh in range(2):
                     for s in range(0, 64, 8):
@@ -315,10 +379,18 @@
                         sent_back[pl.ds(start, 8, stride=CHUNK), :] = result[m : m + 8]
             return 0
 
-        lax.fori_loop(0, 4, block_back, 0)
-        own = piece_copies(sent_back, returned, back_send, back_recv, g)
+        lax.fori_loop(0, 4, block_back, 0, unroll=True)
+        back_copies(g, side, 1)
+        mine = pl.ds(pl.multiple_of(r * CHUNK + g * PIECE, PIECE), PIECE)
+        own = pltpu.make_async_copy(sent_back.at[mine], returned.at[mine], own_sem)
         own.start()
         own.wait()
+        return 0
+
+    def later_piece(g, _):
+        all_of(sent, arrived, send_sem, recv_sem, g).wait_recv()
+        column_piece(g, 0)
+        back_copies(g - 1, 1 - side, 0)
         return 0
 
     lane = lax.broadcasted_iota(jnp.int32, (8, 128), 1)
@@ -359,10 +431,8 @@
     ]
 
     def prior_step():
-        for load in loads[1:3]:
+        for load in loads[4:6]:
             load.wait()
-        for copy in sky_copies:
-            copy.wait_recv()
         for k in range(2):
             remote(far_send.at[0], far_got.at[k], sky_send.at[2], sky_recv.at[2 + k], r, other).wait_recv()
         no_far = jnp.logical_or(
@@ -418,9 +488,6 @@
 
         lax.fori_loop(0, 32, edge, 0)
 
-        for copy in prior_copies:
-            copy.start()
-
 
     def adjoint_step():
         prior_copies[0].wait_recv()
@@ -456,9 +523,13 @@
         for k in range(8):
             close(31, k, carry[k][2])
 
-    lax.fori_loop(0, PRIOR_AFTER, column_piece, 0)
     prior_step()
-    lax.fori_loop(PRIOR_AFTER, PIECES, column_piece, 0)
+    all_of(sent, arrived, send_sem, recv_sem, 0).wait_recv()
+    for copy in prior_copies:
+        copy.start()
+    column_piece(0, 0)
+    lax.fori_loop(1, PIECES, later_piece, 0)
+    back_copies(PIECES - 1, 1 - side, 0)
 
     own_sums[0:1] = jnp.sum(sums[0], axis=0, keepdims=True)
     own_sums[1:2] = jnp.sum(sums[1], axis=0, keepdims=True)
@@ -495,14 +566,14 @@
             for c in range(2):
                 for e in range(2):
                     rows.append(returned[pl.ds(chunk_row(g, c, a_hi, e), PEERS, stride=CHUNK), :])
-            result = gather(jnp.concatenate(rows), gr_ref)
+            result = gather(jnp.concatenate(rows), rows_ref)
             for a_lo in range(16):
                 row = pl.ds(pl.multiple_of((a_hi * 16 + a_lo) * 32 + g * 8, 8), 8)
                 wide[0, row, :] = result[a_lo * 8 : a_lo * 8 + 8, 0:WIDE]
                 wide[1, row, :] = result[a_lo * 8 : a_lo * 8 + 8, WIDE:]
             return 0
 
-        lax.fori_loop(0, 4, block, 0)
+        lax.fori_loop(0, 4, block, 0, unroll=True)
         return 0
 
     lax.fori_loop(0, PIECES, back_piece, 0)
@@ -533,6 +604,16 @@
     lax.fori_loop(0, PIECES, drain, 0)
 
 
+def store(a, b, c, out_a, out_b, out_c, sem):
+    copies = [
+        pltpu.make_async_copy(src, dst, sem.at[i]) for i, (src, dst) in enumerate(((a, out_a), (b, out_b), (c, out_c)))
+    ]
+    for copy in copies:
+        copy.start()
+    for copy in copies:
+        copy.wait()
+
+
 def tiles(array):
     lead, n = array.shape[:-2], array.ndim - 2
     array = array.reshape(lead + (array.shape[-2] // 8, 8, 32, 128))
@@ -550,13 +631,11 @@
     forward, backward = dft_matrix(-1.0), dft_matrix(1.0)
     tables = (
         twiddle(-1.0),
-        high_low(halves_first(forward.T))[0],
+        high_low(halves_first(backward))[0],
         high_low(halves_first(forward))[0],
-        high_low(halves_first(backward.T))[0],
-        high_low(halves_first(backward))[0],
     )
     vmem, dma = pltpu.VMEM, pltpu.SemaphoreType.DMA
-    in_vmem, in_any = pl.BlockSpec(memory_space=pltpu.VMEM), pl.BlockSpec(memory_space=pl.ANY)
+    in_vmem, in_hbm = pl.BlockSpec(memory_space=pltpu.VMEM), pl.BlockSpec(memory_space=pltpu.HBM)
     image, fourier_new, wavelet_new = pl.pallas_call(
         step,
         out_shape=(
@@ -564,29 +643,39 @@
             jax.ShapeDtypeStruct((2, 8, 32, 8, 128), F32),
             jax.ShapeDtypeStruct((2, 4, 32, 8, 128), F32),
         ),
-        in_specs=[pl.BlockSpec(memory_space=pltpu.SMEM)] + [in_any] * 6 + [in_vmem] * 5,
+        in_specs=[pl.BlockSpec(memory_space=pltpu.SMEM)] + [in_hbm] * 9,
         out_specs=(in_vmem,) * 3,
         scratch_shapes=[
             vmem((8, 32, 8, 128), F32), vmem((2, 8, 32, 8, 128), F32), vmem((2, 8, 32, 8, 128), F32),
             vmem((8, 32, 8, 128), F32), vmem((2, 4, 32, 8, 128), F32), vmem((4, 32, 8, 128), F32),
+            vmem((2, RADIX, WIDE), F32), vmem((2, 256, 256), jnp.bfloat16), vmem((2, 256, 256), jnp.bfloat16),
             vmem((4096, 128), F32), vmem((4096, 128), F32), vmem((4096, 128), F32), vmem((4096, 128), F32),
-            vmem((16, 128, 256), F32), vmem((2, 2048, 128), F32),
+            vmem((16, 128, 256), F32), vmem((8, 128, 256), F32), vmem((2048, 128), F32), vmem((2, 2048, 128), F32),
             vmem((2, 8, 128), F32), vmem((2, 128), F32), vmem((PEERS, 2, 128), F32),
             vmem((32, 2, 128), F32), vmem((2, 32, 2, 128), F32),
             vmem((4, 32, 8, 128), F32), vmem((32, 2, 128), F32), vmem((2, 32, 2, 128), F32),
             vmem((2, 32, 48, 128), F32),
             vmem((2, 32, 2, 128), F32), vmem((4, 32, 8, 128), F32), vmem((2, 32, 2, 128), F32),
             vmem((32, 80, 128), F32),
-            dma((6,)), dma, dma((PIECES,)), dma((PIECES,)), dma((PIECES,)), dma((PIECES,)),
+            dma((9,)), dma, dma((PIECES,)), dma((PIECES,)), dma((PIECES,)), dma((PIECES,)),
             dma, dma, dma((4,)), dma((4,)), dma((3,)), dma((3,)),
         ],
         compiler_params=pltpu.CompilerParams(
-            collective_id=0, has_side_effects=True, vmem_limit_bytes=60 << 20
+            collective_id=0, has_side_effects=True, vmem_limit_bytes=VMEM_MIB << 20
         ),
     )(
-        radius, tiles(sky_image[0]), tiles(fourier_dual[:, 0]), tiles(visibilities[:, 0]), tiles(weights[0]),
-        tiles(wavelet_dual), tiles(reweight), *tables,
+        radius, *(pltpu.with_memory_space_constraint(v, pltpu.HBM) for v in (
+            *map(tiles, (sky_image[0], wavelet_dual, reweight, fourier_dual[:, 0], visibilities[:, 0], weights[0])), *tables)),
     )
+    results = (image, fourier_new, wavelet_new)
+    image, fourier_new, wavelet_new = pl.pallas_call(
+        store,
+        out_shape=tuple(jax.ShapeDtypeStruct(v.shape, F32) for v in results),
+        in_specs=[in_vmem] * 3,
+        out_specs=(in_hbm,) * 3,
+        scratch_shapes=[dma((3,))],
+        compiler_params=pltpu.CompilerParams(vmem_limit_bytes=4 << 20),
+    )(*results)
     return (untiles(image)[None], untiles(fourier_new)[:, None], untiles(wavelet_new))
 
 

time: 104 us -> 85.3 us (0.82)
  Pallas kernels: 97.3 us -> 83.9 us
  local copies, waits for them, and re-layouts: 5.35 us -> 0 us
    pallas_call x1, Pallas kernels: 97.3 us -> 81.8 us  [per_device(): pl.pallas_call(step, out_shape=(jax.ShapeDtypeStruct((8, 32, 8, 128), F32...]
    unnamed x7 -> x0, local copies, waits for them, and re-layouts: 5.35 us -> none
    pallas_call x0 -> x1, Pallas kernels: none -> 2.03 us  [per_device(): pl.pallas_call(store, out_shape=tuple((jax.ShapeDtypeStruct(v.shape, F32)...]
where the time goes in v2:
time: 85.3 us; the launch traced here: 85.1 us
  Pallas kernels  83.9 us (98%)
  between operations  1.29 us (2%)
    pallas_call x1, Pallas kernels, per_device(): pl.pallas_call(step, out_shape=(jax.ShapeDtypeStruct((8, 32, 8, 128), F32...  81.8 us
    pallas_call x1, Pallas kernels, per_device(): pl.pallas_call(store, out_shape=tuple((jax.ShapeDtypeStruct(v.shape, F32)...  2.03 us

profile of v2, /device:TPU:1, one launch (start us, length us, event | category | flops | bytes accessed | tf_op | source)
XLA Modules:
  0.0 85.1 jit_solution(408275621422071765)
XLA Ops:
  1.3 81.8 %shard_map.121 = (f32[8,32,8,128]{3,2,1,0:T(8,128)S(1)}, f32[2,8,32,8,128]{4,3,2,1,0:T(8,128)S(1)}, f32[2,4,32,8,128]{4,3,2,1,0:T(8,128)S(1)}) custom-call(f32[1]{0:T(128)S(6)} %copy.13.radius_ref, f32[8,32,8,128]{3,2,1,0:T(8,128)} %bitcast.29, f32[2,4,32,8,128]{4,3,2,1,0:T(8,128)} %bitcast.30, f32[4,32,8,128]{3,2,1,0:T(8,128)} %bitcast.32, ...), custom_call_target="tpu_custom_call" | custom-call | tf_op jit(solution)/shard_map/pallas_call | solution.py:639
  83.1 2.0 %shard_map.122 = (f32[8,32,8,128]{3,2,1,0:T(8,128)}, f32[2,8,32,8,128]{4,3,2,1,0:T(8,128)}, f32[2,4,32,8,128]{4,3,2,1,0:T(8,128)}) custom-call(f32[8,32,8,128]{3,2,1,0:T(8,128)S(1)} %get-tuple-element.9.a, f32[2,8,32,8,128]{4,3,2,1,0:T(8,128)S(1)} %get-tuple-element.10.b, f32[2,4,32,8,128]{4,3,2,1,0:T(8,128)S(1)} %get-tuple-element.11.c), custom_call_target="tpu_custom_call" | custom-call | tf_op jit(solution)/shard_map/pallas_call | solution.py:671

commit v3 on v2

--- a/solution.py
+++ b/solution.py
@@ -134,15 +134,35 @@
 
 def step(
     radius_ref, x_hbm, prior_hbm, limit_hbm, dual_hbm, vis_hbm, weight_hbm, tw_hbm, rows_hbm, columns_hbm,
-    image_ref, fourier_ref, wavelet_ref,
+    image_ref, fourier_ref, wavelet_ref, wide, factor_ref,
     x_ref, dual_ref, vis_ref, weight_ref, prior_ref, limit_ref, tw_ref, rows_ref, columns_ref,
-    sent, arrived, sent_back, returned, held, facet_held, facet_sent, wide, sums, own_sums, all_sums,
+    sent, arrived, sent_back, returned, held, facet_held, facet_sent, sums, own_sums, all_sums,
     near_send, far_send, sky_got, near_got, far_got, grown, edge_send, prior_got, edge_got, spread_new,
     load_sem, own_sem, send_sem, recv_sem, back_send, back_recv, sum_send, sum_recv, sky_send, sky_recv, pri_send, pri_recv,
 ):
     r, ch = lax.axis_index("row"), lax.axis_index("chan")
     other = 1 - ch
     after, before = lax.rem(r + 1, PEERS), lax.rem(r + PEERS - 1, PEERS)
+
+    side, z, low = (r // 8) % 2, r // 16, r % 8
+
+    def peer(i, its_side):
+        return lax.rem(z + i // 8, 4) * 16 + its_side * 8 + lax.rem(low + i % 8, 8)
+
+    barrier = pltpu.get_barrier_semaphore()
+
+    def greet(i, _):
+        pl.semaphore_signal(barrier, inc=1, device_id=(lax.rem(r + i, PEERS), ch), device_id_type=MESH)
+        return 0
+
+    def greet_other(i, _):
+        pl.semaphore_signal(barrier, inc=1, device_id=(peer(i, 1 - side), other), device_id_type=MESH)
+        return 0
+
+    lax.fori_loop(0, PEERS // 2, greet_other, 0)
+    lax.fori_loop(1, PEERS, greet, 0)
+    for row in (after, before, r):
+        pl.semaphore_signal(barrier, inc=1, device_id=(row, other), device_id_type=MESH)
 
     loads = [
         pltpu.make_async_copy(src, dst, load_sem.at[i])
@@ -157,19 +177,6 @@
     for load in loads:
         load.start()
 
-    barrier = pltpu.get_barrier_semaphore()
-
-    def greet_other(i, _):
-        pl.semaphore_signal(barrier, inc=1, device_id=(lax.rem(r + i, PEERS), other), device_id_type=MESH)
-        return 0
-
-    def greet(i, _):
-        pl.semaphore_signal(barrier, inc=1, device_id=(lax.rem(r + i, PEERS), ch), device_id_type=MESH)
-        return 0
-
-    lax.fori_loop(1, PEERS, greet, 0)
-    lax.fori_loop(0, PEERS, greet_other, 0)
-
     def remote(src, dst, send, recv, row, chan):
         return pltpu.make_async_remote_copy(
             src_ref=src, dst_ref=dst, send_sem=send, recv_sem=recv, device_id=(row, chan), device_id_type=MESH
@@ -191,11 +198,6 @@
             into[(q // 8) * blocks + a_hi, row, 0:WIDE] = re
             into[(q // 8) * blocks + a_hi, row, WIDE:] = im
 
-    side, z, low = (r // 8) % 2, r // 16, r % 8
-
-    def peer(i, its_side):
-        return lax.rem(z + i // 8, 4) * 16 + its_side * 8 + lax.rem(low + i % 8, 8)
-
     def row_short(at, _):
         items = [(x_ref[at, p], None) for p in range(RADIX)]
         done = short_fft(items, -1)
@@ -214,7 +216,7 @@
         return 0
 
     lax.fori_loop(0, 32, edges, 0)
-    pl.semaphore_wait(barrier, 2 * PEERS - 1)
+    pl.semaphore_wait(barrier, PEERS - 1 + PEERS // 2 + 3)
 
     half = pl.ds(pl.multiple_of(other * 4, 4), 4)
     sky_copies = [
@@ -543,21 +545,6 @@
     adjoint_step()
     every = pl.ds(0, PEERS - 1)
     told = remote(all_sums.at[every], all_sums.at[every], sum_send, sum_recv, after, ch)
-    told.wait_recv()
-    norms = jnp.sum(all_sums[...], axis=0)
-    resid_norm = jnp.sum(norms[0:1], axis=1, keepdims=True)
-    data_norm = jnp.sum(norms[1:2], axis=1, keepdims=True)
-    shrink = data_step * (1.0 - radius_ref[0] * jnp.sqrt(data_norm) / jnp.sqrt(resid_norm))
-    shrink = jnp.broadcast_to(shrink, (8, 128))
-
-    def scale(i, _):
-        for v in range(32):
-            for part in range(2):
-                fourier_ref[part, i, v] = fourier_ref[part, i, v] * shrink
-        return 0
-
-    lax.fori_loop(0, 8, scale, 0)
-
     def back_piece(g, _):
         all_of(sent_back, returned, back_send, back_recv, g).wait_recv()
 
@@ -578,6 +565,48 @@
 
     lax.fori_loop(0, PIECES, back_piece, 0)
 
+    told.wait_recv()
+    norms = jnp.sum(all_sums[...], axis=0)
+    resid_norm = jnp.sum(norms[0:1], axis=1, keepdims=True)
+    data_norm = jnp.sum(norms[1:2], axis=1, keepdims=True)
+    shrink = data_step * (1.0 - radius_ref[0] * jnp.sqrt(data_norm) / jnp.sqrt(resid_norm))
+    shrink = jnp.broadcast_to(shrink, (8, 128))
+    factor_ref[...] = shrink * primal_step
+
+    def scale(i, _):
+        for v in range(32):
+            for part in range(2):
+                fourier_ref[part, i, v] = fourier_ref[part, i, v] * shrink
+        return 0
+
+    lax.fori_loop(0, 8, scale, 0)
+
+
+    for copy in sky_copies + [far_up, far_down] + prior_copies + [told]:
+        copy.wait_send()
+
+    def drain(g, _):
+        all_of(sent, arrived, send_sem, recv_sem, g).wait_send()
+        all_of(sent_back, returned, back_send, back_recv, g).wait_send()
+        return 0
+
+    lax.fori_loop(0, PIECES, drain, 0)
+
+
+def store(base, fourier, wavelet, wide, factor, tw_hbm, out_image, out_fourier, out_wavelet, image, tw_ref, sem, image_sem):
+    table = pltpu.make_async_copy(tw_hbm, tw_ref, sem.at[2])
+    table.start()
+    copies = [
+        pltpu.make_async_copy(src, dst, sem.at[i])
+        for i, (src, dst) in enumerate(((fourier, out_fourier), (wavelet, out_wavelet)))
+    ]
+    for copy in copies:
+        copy.start()
+    table.wait()
+
+    def image_copy(at):
+        return pltpu.make_async_copy(image.at[at], out_image.at[at], image_sem.at[at])
+
     def finish(at, _):
         items = []
         for q in range(RADIX):
@@ -586,32 +615,16 @@
                 c_mul((wide[0, row, :], wide[1, row, :]), tw_ref[0, pl.ds(q, 1), :], -tw_ref[1, pl.ds(q, 1), :])
             )
         done = short_fft(items, 1)
-        factor = shrink * primal_step
         for p in range(RADIX):
-            image_ref[at, p] = jnp.maximum(image_ref[at, p] - done[p][0] * factor, 0.0)
+            image[at, p] = jnp.maximum(base[at, p] - done[p][0] * factor[...], 0.0)
+        image_copy(at).start()
         return 0
 
     lax.fori_loop(0, 8, finish, 0)
-
-    for copy in sky_copies + [far_up, far_down] + prior_copies + [told]:
-        copy.wait_send()
-
-    def drain(g, _):
-        all_of(sent, arrived, send_sem, recv_sem, g).wait_send()
-        all_of(sent_back, returned, back_send, back_recv, g).wait_send()
-        return 0
-
-    lax.fori_loop(0, PIECES, drain, 0)
-
-
-def store(a, b, c, out_a, out_b, out_c, sem):
-    copies = [
-        pltpu.make_async_copy(src, dst, sem.at[i]) for i, (src, dst) in enumerate(((a, out_a), (b, out_b), (c, out_c)))
-    ]
-    for copy in copies:
-        copy.start()
     for copy in copies:
         copy.wait()
+    for at in range(8):
+        image_copy(at).wait()
 
 
 def tiles(array):
@@ -636,21 +649,23 @@
     )
     vmem, dma = pltpu.VMEM, pltpu.SemaphoreType.DMA
     in_vmem, in_hbm = pl.BlockSpec(memory_space=pltpu.VMEM), pl.BlockSpec(memory_space=pltpu.HBM)
-    image, fourier_new, wavelet_new = pl.pallas_call(
+    results = pl.pallas_call(
         step,
         out_shape=(
             jax.ShapeDtypeStruct((8, 32, 8, 128), F32),
             jax.ShapeDtypeStruct((2, 8, 32, 8, 128), F32),
             jax.ShapeDtypeStruct((2, 4, 32, 8, 128), F32),
+            jax.ShapeDtypeStruct((2, 2048, 128), F32),
+            jax.ShapeDtypeStruct((8, 128), F32),
         ),
         in_specs=[pl.BlockSpec(memory_space=pltpu.SMEM)] + [in_hbm] * 9,
-        out_specs=(in_vmem,) * 3,
+        out_specs=(in_vmem,) * 5,
         scratch_shapes=[
             vmem((8, 32, 8, 128), F32), vmem((2, 8, 32, 8, 128), F32), vmem((2, 8, 32, 8, 128), F32),
             vmem((8, 32, 8, 128), F32), vmem((2, 4, 32, 8, 128), F32), vmem((4, 32, 8, 128), F32),
             vmem((2, RADIX, WIDE), F32), vmem((2, 256, 256), jnp.bfloat16), vmem((2, 256, 256), jnp.bfloat16),
             vmem((4096, 128), F32), vmem((4096, 128), F32), vmem((4096, 128), F32), vmem((4096, 128), F32),
-            vmem((16, 128, 256), F32), vmem((8, 128, 256), F32), vmem((2048, 128), F32), vmem((2, 2048, 128), F32),
+            vmem((16, 128, 256), F32), vmem((8, 128, 256), F32), vmem((2048, 128), F32),
             vmem((2, 8, 128), F32), vmem((2, 128), F32), vmem((PEERS, 2, 128), F32),
             vmem((32, 2, 128), F32), vmem((2, 32, 2, 128), F32),
             vmem((4, 32, 8, 128), F32), vmem((32, 2, 128), F32), vmem((2, 32, 2, 128), F32),
@@ -667,15 +682,14 @@
         radius, *(pltpu.with_memory_space_constraint(v, pltpu.HBM) for v in (
             *map(tiles, (sky_image[0], wavelet_dual, reweight, fourier_dual[:, 0], visibilities[:, 0], weights[0])), *tables)),
     )
-    results = (image, fourier_new, wavelet_new)
     image, fourier_new, wavelet_new = pl.pallas_call(
         store,
-        out_shape=tuple(jax.ShapeDtypeStruct(v.shape, F32) for v in results),
-        in_specs=[in_vmem] * 3,
+        out_shape=tuple(jax.ShapeDtypeStruct(v.shape, F32) for v in results[:3]),
+        in_specs=[in_vmem] * 5 + [in_hbm],
         out_specs=(in_hbm,) * 3,
-        scratch_shapes=[dma((3,))],
-        compiler_params=pltpu.CompilerParams(vmem_limit_bytes=4 << 20),
-    )(*results)
+        scratch_shapes=[vmem((8, 32, 8, 128), F32), vmem((2, RADIX, WIDE), F32), dma((3,)), dma((8,))],
+        compiler_params=pltpu.CompilerParams(vmem_limit_bytes=8 << 20),
+    )(*results, pltpu.with_memory_space_constraint(tables[0], pltpu.HBM))
     return (untiles(image)[None], untiles(fourier_new)[:, None], untiles(wavelet_new))
 
 

time: 85.3 us -> 83.7 us (0.981)
  Pallas kernels: 83.9 us -> 82.2 us
    pallas_call x1, Pallas kernels: 81.8 us -> 78.8 us  [per_device(): pl.pallas_call(step, out_shape=(jax.ShapeDtypeStruct((8, 32, 8, 128), F32...]
    pallas_call x1, Pallas kernels: 2.03 us -> 3.4 us  [per_device(): pl.pallas_call(store, out_shape=tuple((jax.ShapeDtypeStruct(v.shape, F32)...]
where the time goes in v3:
time: 83.7 us; the launch traced here: 83.5 us
  Pallas kernels  82.2 us (98%)
  between operations  1.29 us (2%)
    pallas_call x1, Pallas kernels, per_device(): pl.pallas_call(step, out_shape=(jax.ShapeDtypeStruct((8, 32, 8, 128), F32...  78.8 us
    pallas_call x1, Pallas kernels, per_device(): pl.pallas_call(store, out_shape=tuple((jax.ShapeDtypeStruct(v.shape, F32)...  3.4 us

profile of v3, /device:TPU:1, one launch (start us, length us, event | category | flops | bytes accessed | tf_op | source)
XLA Modules:
  0.0 83.5 jit_solution(6767280575193187418)
XLA Ops:
  1.3 78.8 %shard_map.121 = (f32[8,32,8,128]{3,2,1,0:T(8,128)S(1)}, f32[2,8,32,8,128]{4,3,2,1,0:T(8,128)S(1)}, f32[2,4,32,8,128]{4,3,2,1,0:T(8,128)S(1)}, f32[2,2048,128]{2,1,0:T(8,128)S(1)}, f32[8,128]{1,0:T(8,128)S(1)}) custom-call(f32[1]{0:T(128)S(6)} %copy.13.radius_ref, f32[8,32,8,128]{3,2,1,0:T(8,128)} %bitcast.29, f32[2,4,32,8,128]{4,3,2,1,0:T(8,128)} %bitcast.30, ...), custom_call_target="tpu_custom_call" | custom-call | tf_op jit(solution)/shard_map/pallas_call | solution.py:652
  80.1 3.4 %shard_map.122 = (f32[8,32,8,128]{3,2,1,0:T(8,128)}, f32[2,8,32,8,128]{4,3,2,1,0:T(8,128)}, f32[2,4,32,8,128]{4,3,2,1,0:T(8,128)}) custom-call(f32[8,32,8,128]{3,2,1,0:T(8,128)S(1)} %get-tuple-element.11.base, f32[2,8,32,8,128]{4,3,2,1,0:T(8,128)S(1)} %get-tuple-element.12.fourier, f32[2,4,32,8,128]{4,3,2,1,0:T(8,128)S(1)} %get-tuple-element.13.wavelet, ...), custom_call_target="tpu_custom_call" | custom-call | tf_op jit(solution)/shard_map/pallas_call | solution.py:685

commit v4 on v3

--- a/solution.py
+++ b/solution.py
@@ -430,7 +430,7 @@
             lax.rem(r + PEERS - 1 + 2 * ch, PEERS), c,
         )
         for c in range(2)
-    ]
+    ] + [remote(edge_send.at[2], edge_got.at[2], pri_send.at[3], pri_recv.at[3], r, other)]
 
     def prior_step():
         for load in loads[4:6]:
@@ -486,48 +486,54 @@
                 edge_send[c, t] = jnp.where(
                     first_here, wavelet_ref[c, 0, t][0:2], wavelet_ref[c, 3, t][6:8]
                 )
+            edge_send[2, t] = jnp.where(first_here, wavelet_ref[other, 3, t][6:8], wavelet_ref[other, 0, t][0:2])
             return 0
 
         lax.fori_loop(0, 32, edge, 0)
 
 
-    def adjoint_step():
-        prior_copies[0].wait_recv()
-        for k in range(2):
-            remote(edge_send.at[0], edge_got.at[k], pri_send.at[1], pri_recv.at[1 + k], r, other).wait_recv()
-
+    def adjoint_half(half, rows, near_above, near_below):
         def fill(t, _):
             for k in range(4):
-                mine = pl.ds(pl.multiple_of(8 + ch * 32 + 8 * k, 8), 8)
-                theirs = pl.ds(pl.multiple_of(8 + other * 32 + 8 * k, 8), 8)
-                spread_new[t, mine, :] = wavelet_ref[ch, k, t]
-                spread_new[t, theirs, :] = prior_got[k, t]
-            spread_new[t, 6:8, :] = jnp.where(r == 0, 0.0, edge_got[0, t])
-            spread_new[t, 72:74, :] = jnp.where(r == PEERS - 1, 0.0, edge_got[1, t])
+                spread_new[half, t, 8 + 8 * k : 16 + 8 * k, :] = rows(k, t)
+            above = jnp.where(r == 0, 0.0, edge_got[0, t])
+            below = jnp.where(r == PEERS - 1, 0.0, edge_got[1, t])
+            spread_new[half, t, 6:8, :] = jnp.where(half == 0, above, near_above(t))
+            spread_new[half, t, 40:42, :] = jnp.where(half == 0, near_below(t), below)
             return 0
 
         lax.fori_loop(0, 32, fill, 0)
 
         def close(t, k, filtered):
-            image_ref[k, t] = x_ref[k, t] - primal_step * filtered
+            image_ref[half * 4 + k, t] = x_ref[half * 4 + k, t] - primal_step * filtered
 
         def columns(t, carry):
             new = []
-            for k in range(8):
+            for k in range(4):
                 finished, kept = filter_column(
-                    lambda p: spread_new[t, 6 + 8 * k + p : 14 + 8 * k + p, :], low_reverse, high_reverse, carry[k]
+                    lambda p: spread_new[half, t, 6 + 8 * k + p : 14 + 8 * k + p, :], low_reverse, high_reverse, carry[k]
                 )
                 close(jnp.maximum(t - 1, 0), k, finished)
                 new.append(kept)
             return tuple(new)
 
-        carry = lax.fori_loop(0, 32, columns, ((zero, zero, zero),) * 8)
-        for k in range(8):
+        carry = lax.fori_loop(0, 32, columns, ((zero, zero, zero),) * 4)
+        for k in range(4):
             close(31, k, carry[k][2])
+
+    def adjoint_step():
+        for k in range(3):
+            remote(edge_send.at[0], edge_got.at[k], pri_send.at[1], pri_recv.at[1 + k], r, other).wait_recv()
+        adjoint_half(ch, lambda k, t: wavelet_ref[ch, k, t], lambda t: edge_got[2, t], lambda t: edge_got[2, t])
+        prior_copies[0].wait_recv()
+        adjoint_half(
+            other, lambda k, t: prior_got[k, t],
+            lambda t: wavelet_ref[ch, 3, t][6:8], lambda t: wavelet_ref[ch, 0, t][0:2],
+        )
 
     prior_step()
     all_of(sent, arrived, send_sem, recv_sem, 0).wait_recv()
-    for copy in prior_copies:
+    for copy in prior_copies[1:] + prior_copies[:1]:
         copy.start()
     column_piece(0, 0)
     lax.fori_loop(1, PIECES, later_piece, 0)
@@ -670,10 +676,10 @@
             vmem((32, 2, 128), F32), vmem((2, 32, 2, 128), F32),
             vmem((4, 32, 8, 128), F32), vmem((32, 2, 128), F32), vmem((2, 32, 2, 128), F32),
             vmem((2, 32, 48, 128), F32),
-            vmem((2, 32, 2, 128), F32), vmem((4, 32, 8, 128), F32), vmem((2, 32, 2, 128), F32),
-            vmem((32, 80, 128), F32),
+            vmem((3, 32, 2, 128), F32), vmem((4, 32, 8, 128), F32), vmem((3, 32, 2, 128), F32),
+            vmem((2, 32, 48, 128), F32),
             dma((9,)), dma, dma((PIECES,)), dma((PIECES,)), dma((PIECES,)), dma((PIECES,)),
-            dma, dma, dma((4,)), dma((4,)), dma((3,)), dma((3,)),
+            dma, dma, dma((4,)), dma((4,)), dma((4,)), dma((4,)),
         ],
         compiler_params=pltpu.CompilerParams(
             collective_id=0, has_side_effects=True, vmem_limit_bytes=VMEM_MIB << 20

time: 83.7 us -> 82.9 us (level)
  no operation moved by 1% of the time
where the time goes in v4:
time: 82.9 us; the launch traced here: 82.7 us
  Pallas kernels  81.4 us (98%)
  between operations  1.29 us (2%)
    pallas_call x1, Pallas kernels, per_device(): pl.pallas_call(step, out_shape=(jax.ShapeDtypeStruct((8, 32, 8, 128), F32...  78 us
    pallas_call x1, Pallas kernels, per_device(): pl.pallas_call(store, out_shape=tuple((jax.ShapeDtypeStruct(v.shape, F32)...  3.4 us

profile of v4, /device:TPU:1, one launch (start us, length us, event | category | flops | bytes accessed | tf_op | source)
XLA Modules:
  0.0 82.7 jit_solution(12742656347176795311)
XLA Ops:
  1.3 78.0 %shard_map.121 = (f32[8,32,8,128]{3,2,1,0:T(8,128)S(1)}, f32[2,8,32,8,128]{4,3,2,1,0:T(8,128)S(1)}, f32[2,4,32,8,128]{4,3,2,1,0:T(8,128)S(1)}, f32[2,2048,128]{2,1,0:T(8,128)S(1)}, f32[8,128]{1,0:T(8,128)S(1)}) custom-call(f32[1]{0:T(128)S(6)} %copy.13.radius_ref, f32[8,32,8,128]{3,2,1,0:T(8,128)} %bitcast.29, f32[2,4,32,8,128]{4,3,2,1,0:T(8,128)} %bitcast.30, ...), custom_call_target="tpu_custom_call" | custom-call | tf_op jit(solution)/shard_map/pallas_call | solution.py:658
  79.3 3.4 %shard_map.122 = (f32[8,32,8,128]{3,2,1,0:T(8,128)}, f32[2,8,32,8,128]{4,3,2,1,0:T(8,128)}, f32[2,4,32,8,128]{4,3,2,1,0:T(8,128)}) custom-call(f32[8,32,8,128]{3,2,1,0:T(8,128)S(1)} %get-tuple-element.11.base, f32[2,8,32,8,128]{4,3,2,1,0:T(8,128)S(1)} %get-tuple-element.12.fourier, f32[2,4,32,8,128]{4,3,2,1,0:T(8,128)S(1)} %get-tuple-element.13.wavelet, ...), custom_call_target="tpu_custom_call" | custom-call | tf_op jit(solution)/shard_map/pallas_call | solution.py:691
